TPU v7x, 32 devices: a whole 2x2x4 slice. The times are simulated.
32 devices in a mesh: fsdp: 4 (over z), replica: 2 (over x), tensor: 4 (over y, core).
Axes of the slice: x: 2, y: 2, z: 4, core: 2. Of those that a mesh axis runs over, the one named last changes fastest.
Arguments:
- tokens: bfloat16 [1024, 8192], P(('fsdp', 'replica')), may hold values from -6 to 6
- weight_codes: bfloat16 [8192, 14336], P('fsdp', 'tensor'), may hold values from -127 to 127, as said below
- scales: float32 [64, 14336], P('fsdp', 'tensor'), may hold values from 3e-05 to 0.0003
- cotangent: bfloat16 [1024, 14336], P(('fsdp', 'replica'), 'tensor'), may hold values from -6 to 6
- sign_bits: int32 [14336], P('tensor'), may hold values from 0 to 1
Outputs:
- activation: bfloat16 [1024, 14336], P(('fsdp', 'replica'), 'tensor')
- input_grad: bfloat16 [1024, 8192], P(('fsdp', 'replica'), 'tensor')
- grad_codes: float32 [8192, 14336], P(('fsdp', 'replica'), 'tensor')
Inputs may be any that keep to these rules, and one draw needn't show every extreme that they name: `weight_codes`: integer values, held exactly.
All inputs are finite; a program needn't handle non-finite values.
Results may differ from a plain program's by a relative error of at most 0.015.
Values may be sent and summed in bfloat16 or wider, within the bound.
A program may use at most 128 MiB of HBM per device.

v0:
```python
import jax
import jax.numpy as jnp
from jax import lax
from jax.sharding import PartitionSpec as P

HB = 128


def hadamard_table(length):
    indices = jnp.arange(length, dtype=jnp.int32)
    intersection_bits = jnp.bitwise_and(indices[:, None], indices[None, :])
    parity = jnp.zeros((length, length), jnp.int32)
    for bit_pos in range(length.bit_length() - 1):
        parity = parity + jnp.bitwise_and(jnp.right_shift(intersection_bits, bit_pos), 1)
    return (1 - 2 * (parity % 2)).astype(jnp.float32)


def rotate_blocks(matrix, sign_bits, scaling):
    height, width = matrix.shape
    signed = matrix * (2 * sign_bits - 1).astype(jnp.float32)[None, :]
    blocks = signed.reshape(height, width // HB, HB)
    turned = jnp.einsum("rbi,ij->rbj", blocks, hadamard_table(HB), precision=lax.Precision.HIGHEST)
    return turned.reshape(height, width) * scaling


def shards(tokens, weight_codes, scales, cotangent, sign_bits):
    local_tokens = tokens.shape[0]
    shard_rows, hidden_cols = weight_codes.shape
    block_rows = shard_rows // scales.shape[0]
    weight = (
        (
            weight_codes.astype(jnp.float32).reshape(scales.shape[0], block_rows, hidden_cols)
            * scales[:, None, :]
        )
        .reshape(shard_rows, hidden_cols)
        .astype(jnp.bfloat16)
    )
    columns = lax.all_to_all(tokens, "fsdp", split_axis=1, concat_axis=0, tiled=True)
    token_rows = columns
    hidden = lax.psum_scatter(
        jnp.dot(token_rows, weight, preferred_element_type=jnp.float32).astype(jnp.bfloat16),
        "fsdp",
        scatter_dimension=0,
        tiled=True,
    ).astype(jnp.float32)
    sigmoid_val = jax.nn.sigmoid(hidden)
    activation = (hidden * sigmoid_val).astype(jnp.bfloat16)
    hidden_grad = (
        cotangent.astype(jnp.float32) * sigmoid_val * (1.0 + hidden * (1.0 - sigmoid_val))
    ).astype(jnp.bfloat16)
    arrived = lax.all_gather(hidden_grad, "fsdp", axis=0, tiled=True)
    token_rows = columns
    weight_grad = lax.dot_general(
        token_rows, arrived, (((0,), (0,)), ((), ())), preferred_element_type=jnp.float32
    )
    product = lax.dot_general(
        arrived, weight, (((1,), (1,)), ((), ())), preferred_element_type=jnp.float32
    ).astype(jnp.bfloat16)
    input_rows = product
    weight_grad, input_rows = (weight_grad, input_rows)
    returned = lax.all_to_all(input_rows, "fsdp", split_axis=0, concat_axis=1, tiled=True)
    input_grad = lax.psum_scatter(
        returned.astype(jnp.float32).astype(jnp.bfloat16), "tensor", scatter_dimension=1, tiled=True
    )
    total_tokens = local_tokens * lax.axis_size("fsdp") * lax.axis_size("replica")
    scaling = 1.0 / jnp.sqrt(jnp.float32(HB) * jnp.float32(total_tokens))
    grad_codes = rotate_blocks(
        lax.psum_scatter(
            weight_grad.astype(jnp.bfloat16), "replica", scatter_dimension=0, tiled=True
        ).astype(jnp.float32),
        sign_bits,
        scaling,
    )
    return (activation, input_grad, grad_codes)


def solution(mesh):
    return jax.shard_map(
        shards,
        mesh=mesh,
        in_specs=(
            P(("fsdp", "replica"), None),
            P("fsdp", "tensor"),
            P("fsdp", "tensor"),
            P(("fsdp", "replica"), "tensor"),
            P("tensor"),
        ),
        out_specs=(
            P(("fsdp", "replica"), "tensor"),
            P(("fsdp", "replica"), "tensor"),
            P(("fsdp", "replica"), "tensor"),
        ),
        check_vma=False,
    )
```

profile of v0, /device:TPU:4, one launch (start us, length us, event | category | flops | bytes accessed | tf_op | source)
XLA Modules:
  0.0 461.8 jit_solution(12384013270102566466)
XLA Ops:
  7.2 0.0 copy-start.1
  7.2 4.1 copy.25
  11.3 4.9 %all-to-all-start = ((bf16[128,4,2048]{0,2,1:T(8,128)(2,1)}), bf16[128,4,2048]{0,2,1:T(8,128)(2,1)S(1)}, u32[]{:S(2)}, u32[]{:S(2)}) async-start(bf16[128,4,2048]{0,2,1:T(8,128)(2,1)} %bitcast.32), calls=%async_computation | async-start | bytes 4194304 | tf_op jit(solution)/shard_map/all_to_all | solution.py:38
  16.2 0.0 reduce-scatter.10.cloned.1.call-start
  16.2 0.0 copy-done.1
  16.2 14.0 %fusion = bf16[2048,3584]{1,0:T(8,128)(2,1)} fusion(bf16[2048,3584]{1,0:T(8,128)(2,1)} %param.6, f32[16,3584]{1,0:T(8,128)S(1)} %copy-done.1), kind=kLoop, calls=%fused_computation.1 | loop fusion | flops 22020096 | bytes 29589504 | tf_op jit(solution)/shard_map/convert_element_type | solution.py:36
  30.2 34.2 %all-to-all-done = bf16[128,4,2048]{0,2,1:T(8,128)(2,1)S(1)} async-done(((bf16[128,4,2048]{0,2,1:T(8,128)(2,1)}), bf16[128,4,2048]{0,2,1:T(8,128)(2,1)S(1)}, u32[]{:S(2)}, u32[]{:S(2)}) %all-to-all-start) | async-done | bytes 2097184 | tf_op jit(solution)/shard_map/all_to_all | solution.py:38
  64.4 2.7 copy.26
  67.0 13.0 %fusion.2 = bf16[512,3584]{0,1:T(8,128)(2,1)} fusion(bf16[2048,3584]{1,0:T(8,128)(2,1)} %fusion, bf16[512,2048]{1,0:T(8,128)(2,1)} %bitcast.34), kind=kOutput, calls=%fused_computation.7 | convolution fusion | flops 7518027776 | bytes 20447232 | tf_op jit(solution)/shard_map/dot_general | solution.py:41
  80.1 6.0 %copy.33 = bf16[512,3584]{1,0:T(8,128)(2,1)} copy(bf16[512,3584]{0,1:T(8,128)(2,1)} %fusion.2) | data formatting | bytes 7340032
  86.0 0.0 copy-start
  86.0 0.0 reduce-scatter.10.cloned.1.call-update
  86.1 0.0 all-gather.2.cloned.1.call-start
  86.1 1.1 copy-done
  87.2 0.6 copy.27
  87.8 66.0 %reduce-scatter.10.cloned.1.call-done = bf16[128,3584]{1,0:T(8,128)(2,1)} async-done(((bf16[512,3584]{1,0:T(8,128)(2,1)}), bf16[128,3584]{1,0:T(8,128)(2,1)}) %reduce-scatter.10.cloned.1.call-update) | async-done | bytes 917520
  153.8 1.5 copy.34
  155.4 1.8 fusion.9
  157.2 0.0 all-gather.2.cloned.1.call-update
  157.2 0.0 reduce-scatter.8.cloned.1.call-start
  157.3 72.3 %all-gather.2.cloned.1.call-done = bf16[512,3584]{0,1:T(8,128)(2,1)} async-done(((bf16[128,3584]{0,1:T(8,128)(2,1)}), bf16[512,3584]{0,1:T(8,128)(2,1)}) %all-gather.2.cloned.1.call-update) | async-done | bytes 3670032 | tf_op jit(solution)/shard_map/all_gather | solution.py:51
  229.6 13.1 %fusion.1 = bf16[2048,3584]{0,1:T(8,128)(2,1)} fusion(bf16[512,3584]{0,1:T(8,128)(2,1)} %all-gather.2.cloned.1.call-done, bf16[512,2048]{1,0:T(8,128)(2,1)} %bitcast.35), kind=kOutput, calls=%fused_computation.4 | convolution fusion | flops 7523532800 | bytes 20447232 | tf_op jit(solution)/shard_map/dot_general | solution.py:53
  242.7 0.0 reduce-scatter.8.cloned.1.call-update
  242.7 0.2 reduce-scatter.6.cloned.1.call-start
  243.0 12.2 %convolution_convert_fusion.2 = bf16[512,2048]{1,0:T(8,128)(2,1)S(1)} fusion(bf16[512,3584]{0,1:T(8,128)(2,1)} %all-gather.2.cloned.1.call-done, bf16[2048,3584]{1,0:T(8,128)(2,1)} %fusion), kind=kOutput, calls=%fused_computation.8 | convolution fusion | flops 7517241344 | bytes 20447232 | tf_op jit(solution)/shard_map/dot_general | solution.py:56
  255.2 51.0 %all_to_all.38 = bf16[4,128,2048]{2,1,0:T(8,128)(2,1)S(1)} all-to-all(bf16[4,128,2048]{2,1,0:T(8,128)(2,1)S(1)} %bitcast.36), channel_id=1, replica_groups=mesh['fsdp'=4,'replica'=2,'tensor'=4] {'fsdp'}, dimensions={0} | all-to-all | bytes 4194304 | tf_op jit(solution)/shard_map/all_to_all | solution.py:61
  306.2 0.0 copy-start.2
  306.2 1.5 copy.35
  307.6 0.0 reduce-scatter.6.cloned.1.call-update
  307.7 0.0 copy-done.2
  307.7 1.3 copy.30
  309.0 99.3 %reduce-scatter.8.cloned.1.call-done = bf16[1024,3584]{0,1:T(8,128)(2,1)} async-done(((bf16[2048,3584]{0,1:T(8,128)(2,1)}), bf16[1024,3584]{0,1:T(8,128)(2,1)}) %reduce-scatter.8.cloned.1.call-update) | async-done | bytes 7340048 | tf_op jit(solution)/shard_map/reduce_scatter | solution.py:68
  408.2 9.6 %convert_multiply_fusion = f32[1024,3584]{0,1:T(8,128)} fusion(bf16[1024,3584]{0,1:T(8,128)(2,1)} %reduce-scatter.8.cloned.1.call-done, f32[3584]{0:T(1024)S(1)} %add_convert_fusion), kind=kLoop, calls=%fused_computation.3 | loop fusion | flops 7340032 | bytes 22034432 | tf_op jit(solution)/shard_map/mul | solution.py:20
  417.8 23.1 %convolution_multiply_fusion = f32[1024,28,128]{0,2,1:T(8,128)} fusion(f32[1024,28,128]{0,2,1:T(8,128)} %bitcast.29), kind=kOutput, calls=%fused_computation.5 | convolution fusion | flops 5641388032 | bytes 29360128 | tf_op jit(solution)/shard_map/rbi,ij->rbj/dot_general | solution.py:22
  441.0 14.3 %copy.31 = f32[1024,3584]{1,0:T(8,128)} copy(f32[1024,3584]{0,1:T(8,128)} %bitcast.28) | data formatting | bytes 29360128
  455.2 0.0 reduce-scatter.6.cloned.1.call-done
  (1 shorter events, 0.0 us)
Async XLA Ops:
  7.2 9.0 %copy-start.1 = (f32[16,3584]{1,0:T(8,128)S(1)}, f32[16,3584]{1,0:T(8,128)}, u32[]{:S(2)}) copy-start(f32[16,3584]{1,0:T(8,128)} %param.7) | copy-start | bytes 688132
  11.3 53.1 %all-to-all-start = ((bf16[128,4,2048]{0,2,1:T(8,128)(2,1)}), bf16[128,4,2048]{0,2,1:T(8,128)(2,1)S(1)}, u32[]{:S(2)}, u32[]{:S(2)}) async-start(bf16[128,4,2048]{0,2,1:T(8,128)(2,1)} %bitcast.32), calls=%async_computation | async-start | bytes 4194304 | tf_op jit(solution)/shard_map/all_to_all | solution.py:38
  16.2 137.7 %reduce-scatter.10.cloned.1.call-start = ((), (), s32[]{:S(2)}) async-start(), calls=%async_computation.8 | async-start | bytes 4587520
  86.0 1.2 copy-start
  86.1 143.5 %all-gather.2.cloned.1.call-start = ((), (), s32[]{:S(2)}) async-start(), calls=%async_computation.5 | async-start | bytes 4587520 | tf_op jit(solution)/shard_map/all_gather | solution.py:51
  157.2 251.0 %reduce-scatter.8.cloned.1.call-start = ((), (), s32[]{:S(2)}) async-start(), calls=%async_computation.7 | async-start | bytes 22020096 | tf_op jit(solution)/shard_map/reduce_scatter | solution.py:68
  242.7 212.5 %reduce-scatter.6.cloned.1.call-start = ((), (), s32[]{:S(2)}) async-start(), calls=%async_computation.6 | async-start | bytes 2621440 | tf_op jit(solution)/shard_map/reduce_scatter | solution.py:62
  306.2 1.5 copy-start.2
Sparse Core Ops, SparseCore 0:
  86.2 67.6 reduce-scatter.9
  157.3 72.1 all-gather.1
  242.9 165.3 reduce-scatter.7
  411.2 30.0 reduce-scatter.5
where the time goes:
time: 464 us; the launch traced here: 462 us
  waiting for transfers between devices  272 us (59%)
  matrix products  61.5 us (13%)
  blocking collectives  51 us (11%)
  local copies, waits for them, and re-layouts  33 us (7%)
  other arithmetic  25.4 us (5%)
  between operations  13.8 us (3%)
  starting transfers between devices  5.18 us (1%)
    reduce_scatter x1, waiting for transfers between devices, shards(): lax.psum_scatter(weight_grad.astype(jnp.bfloat16), 'replica', scatter_dim...  99.3 us
    all_gather x1, waiting for transfers between devices, shards(): arrived = lax.all_gather(hidden_grad, 'fsdp', axis=0, tiled=True)  72.3 us
    unnamed x5, waiting for transfers between devices  66.1 us
    all_to_all x1, blocking collectives, shards(): lax.all_to_all(input_rows, 'fsdp', split_axis=0, concat_axis=1, tiled=True)  51 us
    all_to_all x1, waiting for transfers between devices, shards(): lax.all_to_all(tokens, 'fsdp', split_axis=1, concat_axis=0, tiled=True)  34.2 us
    unnamed x12, local copies, waits for them, and re-layouts  28.9 us
    dot_general x1, matrix products, rotate_blocks(): jnp.einsum('rbi,ij->rbj', blocks, hadamard_table(HB), precision=lax.Preci...  23.1 us
    convert_element_type x1, other arithmetic, shards(): weight = (weight_codes.astype(jnp.float32).reshape(scales.shape[0], block...  14 us
  transfers between devices with their start and end apart: 5, of which 4 were waited for; matrix products, arithmetic and copies ran while one was open for 17% of the time, Pallas kernels for 0%

commit v1 on v0

v1 whole, which is shorter than its diff:
```python
import functools

import jax
import jax.numpy as jnp
from jax import lax
from jax.experimental import pallas as pl
from jax.experimental.pallas import tpu as pltpu
from jax.sharding import PartitionSpec as P

HB = 128


def hadamard_table(length):
    indices = jnp.arange(length, dtype=jnp.int32)
    intersection_bits = jnp.bitwise_and(indices[:, None], indices[None, :])
    parity = jnp.zeros((length, length), jnp.int32)
    for bit_pos in range(length.bit_length() - 1):
        parity = parity + jnp.bitwise_and(jnp.right_shift(intersection_bits, bit_pos), 1)
    return (1 - 2 * (parity % 2)).astype(jnp.bfloat16)


def grad_kernel(scaling, turned_ref, mine_ref, other_ref, sign_ref, table_ref, out_ref, rotated):
    half, width = mine_ref.shape
    for part, ref in enumerate((mine_ref, other_ref)):
        for block in range(width // HB):
            cols = slice(block * HB, (block + 1) * HB)
            signed = ref[:, cols] * sign_ref[:, cols]
            rotated[part * half:(part + 1) * half, cols] = jnp.dot(
                signed, table_ref[...], preferred_element_type=jnp.float32
            ).astype(jnp.bfloat16)
    out_ref[...] = scaling * jnp.dot(turned_ref[...], rotated[...], preferred_element_type=jnp.float32)


def rotated_grad(turned, mine, other, sign_bits):
    rows, total = turned.shape
    half, width = mine.shape
    tile = next(t for t in (512, 256, HB) if width % t == 0)
    signs = (2 * sign_bits - 1).astype(jnp.bfloat16)[None, :]
    scaling = float(1.0 / (HB * total) ** 0.5)
    column = lambda c: (0, c)
    fixed = lambda c: (0, 0)
    return pl.pallas_call(
        functools.partial(grad_kernel, scaling),
        grid=(width // tile,),
        out_shape=jax.ShapeDtypeStruct((rows, width), jnp.float32),
        in_specs=[
            pl.BlockSpec((rows, total), fixed),
            pl.BlockSpec((half, tile), column),
            pl.BlockSpec((half, tile), column),
            pl.BlockSpec((1, tile), column),
            pl.BlockSpec((HB, HB), fixed),
        ],
        out_specs=pl.BlockSpec((rows, tile), column),
        scratch_shapes=[pltpu.VMEM((total, tile), jnp.bfloat16)],
        compiler_params=pltpu.CompilerParams(vmem_limit_bytes=48 * 1024 * 1024),
        cost_estimate=pl.CostEstimate(
            flops=2 * rows * total * width, bytes_accessed=4 * rows * width + 2 * total * width, transcendentals=0
        ),
        name="rotated_grad",
    )(turned, mine, other, signs, hadamard_table(HB))


def partner(array):
    return lax.ppermute(array, "replica", [(0, 1), (1, 0)])


def shards(tokens, weight_codes, scales, cotangent, sign_bits):
    n_fsdp, n_tensor = lax.axis_size("fsdp"), lax.axis_size("tensor")
    local_tokens = tokens.shape[0]
    shard_rows, hidden_cols = weight_codes.shape
    block_rows = shard_rows // scales.shape[0]
    weight = (
        (
            weight_codes.astype(jnp.float32).reshape(scales.shape[0], block_rows, hidden_cols)
            * scales[:, None, :]
        )
        .reshape(shard_rows, hidden_cols)
        .astype(jnp.bfloat16)
    )
    piece = shard_rows // n_tensor
    own = lax.dynamic_slice_in_dim(
        tokens.reshape(local_tokens, n_fsdp, shard_rows), lax.axis_index("tensor") * piece, piece, 2
    ).reshape(local_tokens, n_fsdp * piece)
    quarter = lax.all_to_all(own, "fsdp", split_axis=1, concat_axis=0, tiled=True)
    columns = lax.all_gather(quarter, "tensor", axis=1, tiled=True)
    half_rows = shard_rows // 2
    replica = lax.axis_index("replica")
    kept = lax.dynamic_slice_in_dim(columns, replica * half_rows, half_rows, 1)
    sent = lax.dynamic_slice_in_dim(columns, (1 - replica) * half_rows, half_rows, 1)
    turned = jnp.concatenate([kept, partner(sent)], axis=0).T
    hidden = lax.psum_scatter(
        jnp.dot(columns, weight, preferred_element_type=jnp.float32).astype(jnp.bfloat16),
        "fsdp",
        scatter_dimension=0,
        tiled=True,
    ).astype(jnp.float32)
    sigmoid_val = jax.nn.sigmoid(hidden)
    activation = (hidden * sigmoid_val).astype(jnp.bfloat16)
    hidden_grad = (
        cotangent.astype(jnp.float32) * sigmoid_val * (1.0 + hidden * (1.0 - sigmoid_val))
    ).astype(jnp.bfloat16)
    arrived = lax.all_gather(hidden_grad, "fsdp", axis=0, tiled=True)
    other = partner(arrived)
    product = lax.dot_general(
        arrived, weight, (((1,), (1,)), ((), ())), preferred_element_type=jnp.float32
    ).astype(jnp.bfloat16)
    if n_fsdp == n_tensor:
        summed = lax.psum_scatter(product, "tensor", scatter_dimension=0, tiled=True)
        swap = [(f * n_tensor + t, t * n_tensor + f) for f in range(n_fsdp) for t in range(n_tensor)]
        input_grad = lax.ppermute(summed, ("fsdp", "tensor"), swap)
    else:
        returned = lax.all_to_all(product, "fsdp", split_axis=0, concat_axis=1, tiled=True)
        input_grad = lax.psum_scatter(returned, "tensor", scatter_dimension=1, tiled=True)
    grad_codes = rotated_grad(turned, arrived, other, sign_bits)
    return (activation, input_grad, grad_codes)


def solution(mesh):
    return jax.shard_map(
        shards,
        mesh=mesh,
        in_specs=(
            P(("fsdp", "replica"), None),
            P("fsdp", "tensor"),
            P("fsdp", "tensor"),
            P(("fsdp", "replica"), "tensor"),
            P("tensor"),
        ),
        out_specs=(
            P(("fsdp", "replica"), "tensor"),
            P(("fsdp", "replica"), "tensor"),
            P(("fsdp", "replica"), "tensor"),
        ),
        check_vma=False,
    )
```

time: 464 us -> 361 us (0.78)
  matrix products: 61.5 us -> 26.2 us
  blocking collectives: 51 us -> 19.3 us
  local copies, waits for them, and re-layouts: 33 us -> 7.14 us
  waiting for transfers between devices: 272 us -> 257 us
  Pallas kernels: 0 us -> 13.2 us
  other arithmetic: 25.4 us -> 17.8 us
    ppermute x0 -> x3, waiting for transfers between devices: none -> 108 us  [the longest x2 100 us: partner(): return lax.ppermute(array, 'replica', [(0, 1), (1, 0)])]
    unnamed x5 -> x4, waiting for transfers between devices: 66.1 us -> 0.07 us
    dot_general x3 -> x1, matrix products: 49.3 us -> 13 us  [shards(): jnp.dot(columns, weight, preferred_element_type=jnp.float32)]
    all_to_all x1 -> x0, waiting for transfers between devices: 34.2 us -> none  [shards(): lax.all_to_all(tokens, 'fsdp', split_axis=1, concat_axis=0, tiled=True)]
    all_to_all x1, blocking collectives: 51 us -> 19.3 us  [shards(): lax.all_to_all(own, 'fsdp', split_axis=1, concat_axis=0, tiled=True)]
    reduce_scatter x2, waiting for transfers between devices: 99.3 us -> 69.8 us  [the longest x1 69.8 us: shards(): lax.psum_scatter(jnp.dot(columns, weight, preferred_element_type=jnp.floa...]
    unnamed x12, local copies, waits for them, and re-layouts: 28.9 us -> 6.1 us
    pallas_call x0 -> x1, Pallas kernels: none -> 13.2 us  [rotated_grad(): pl.pallas_call(functools.partial(grad_kernel, scaling), grid=(width // ti...]
  transfers between devices with their start and end apart: 5 -> 7, of which waited for: 4 -> 5; matrix products, arithmetic and copies ran while one was open for 17% -> 4% of each run, Pallas kernels for 0% -> 4%
where the time goes in v1:
time: 361 us
  waiting for transfers between devices  257 us (71%)
  matrix products  26.2 us (7%)
  blocking collectives  19.3 us (5%)
  other arithmetic  17.8 us (5%)
  between operations  13.9 us (4%)
  Pallas kernels  13.2 us (4%)
  local copies, waits for them, and re-layouts  7.14 us (2%)
  starting transfers between devices  6.1 us (2%)
    ppermute x2, waiting for transfers between devices, partner(): return lax.ppermute(array, 'replica', [(0, 1), (1, 0)])  100 us
    all_gather x1, waiting for transfers between devices, shards(): arrived = lax.all_gather(hidden_grad, 'fsdp', axis=0, tiled=True)  72.4 us
    reduce_scatter x1, waiting for transfers between devices, shards(): lax.psum_scatter(jnp.dot(columns, weight, preferred_element_type=jnp.floa...  69.8 us
    all_to_all x1, blocking collectives, shards(): lax.all_to_all(own, 'fsdp', split_axis=1, concat_axis=0, tiled=True)  19.3 us
    convert_element_type x1, other arithmetic, shards(): weight = (weight_codes.astype(jnp.float32).reshape(scales.shape[0], block...  14.1 us
    pallas_call x1, Pallas kernels, rotated_grad(): pl.pallas_call(functools.partial(grad_kernel, scaling), grid=(width // ti...  13.2 us
    dot_general x1, matrix products, shards(): lax.dot_general(arrived, weight, (((1,), (1,)), ((), ())), preferred_elem...  13.1 us
    dot_general x1, matrix products, shards(): jnp.dot(columns, weight, preferred_element_type=jnp.float32)  13 us
  transfers between devices with their start and end apart: 7, of which 5 were waited for; matrix products, arithmetic and copies ran while one was open for 4% of the time, Pallas kernels for 4%

profile of v1, /device:TPU:4, one launch (start us, length us, event | category | flops | bytes accessed | tf_op | source)
XLA Modules:
  0.0 360.8 jit_solution(5230428697405606894)
XLA Ops:
  7.2 0.0 all-gather.3.cloned.1.call-start
  7.2 3.2 copy.9
  10.4 0.0 copy-start.3
  10.5 19.3 %all_to_all.16 = bf16[128,4,512]{0,2,1:T(8,128)(2,1)S(1)} all-to-all(bf16[128,4,512]{0,2,1:T(8,128)(2,1)S(1)} %constant_dynamic-slice_fusion.2), channel_id=1, replica_groups=mesh['fsdp'=4,'replica'=2,'tensor'=4] {'fsdp'}, dimensions={1} | all-to-all | bytes 1048576 | tf_op jit(solution)/shard_map/all_to_all | solution.py:84
  29.8 0.9 copy_bitcast_fusion
  30.7 0.0 all-gather.3.cloned.1.call-update
  30.7 0.0 reduce-scatter.3.cloned.1.call-start
  30.7 0.0 copy-done.3
  30.7 14.1 %fusion = bf16[2048,3584]{1,0:T(8,128)(2,1)} fusion(bf16[2048,3584]{1,0:T(8,128)(2,1)} %param.6, f32[16,3584]{1,0:T(8,128)S(1)} %copy-done.3), kind=kLoop, calls=%fused_computation.1 | loop fusion | flops 22020096 | bytes 29589504 | tf_op jit(solution)/shard_map/convert_element_type | solution.py:78
  44.9 6.5 %all-gather.3.cloned.1.call-done = bf16[512,2048]{0,1:T(8,128)(2,1)} async-done(((bf16[512,512]{0,1:T(8,128)(2,1)}), bf16[512,2048]{0,1:T(8,128)(2,1)}) %all-gather.3.cloned.1.call-update) | async-done | bytes 2097168 | tf_op jit(solution)/shard_map/all_gather | solution.py:85
  51.3 13.0 %convolution_convert_fusion = bf16[512,3584]{1,0:T(8,128)(2,1)} fusion(bf16[512,2048]{0,1:T(8,128)(2,1)} %all-gather.3.cloned.1.call-done, bf16[2048,3584]{1,0:T(8,128)(2,1)} %fusion), kind=kOutput, calls=%fused_computation.2 | convolution fusion | flops 7518027776 | bytes 20447232 | tf_op jit(solution)/shard_map/dot_general | solution.py:92
  64.4 0.0 copy-start.2
  64.4 0.0 reduce-scatter.3.cloned.1.call-update
  64.4 0.0 all-gather.5.cloned.1.call-start
  64.5 69.8 %reduce-scatter.3.cloned.1.call-done = bf16[128,3584]{1,0:T(8,128)(2,1)} async-done(((bf16[512,3584]{1,0:T(8,128)(2,1)}), bf16[128,3584]{1,0:T(8,128)(2,1)}) %reduce-scatter.3.cloned.1.call-update) | async-done | bytes 917520 | tf_op jit(solution)/shard_map/reduce_scatter | solution.py:91
  134.3 0.0 copy-done.2
  134.3 3.3 fusion.7
  137.5 0.0 all-gather.5.cloned.1.call-update
  137.6 0.0 reduce-scatter.5.cloned.1.call-start
  137.6 72.4 %all-gather.5.cloned.1.call-done.mine_ref = bf16[512,3584]{1,0:T(8,128)(2,1)} async-done(((bf16[128,3584]{1,0:T(8,128)(2,1)}), bf16[512,3584]{1,0:T(8,128)(2,1)}) %all-gather.5.cloned.1.call-update) | async-done | bytes 3670032 | tf_op jit(solution)/shard_map/all_gather | solution.py:102
  210.1 13.1 %convolution_convert_fusion.1 = bf16[512,2048]{1,0:T(8,128)(2,1)} fusion(bf16[512,3584]{1,0:T(8,128)(2,1)} %all-gather.5.cloned.1.call-done.mine_ref, bf16[2048,3584]{1,0:T(8,128)(2,1)} %fusion), kind=kOutput, calls=%fused_computation.3 | convolution fusion | flops 7517241344 | bytes 20447232 | tf_op jit(solution)/shard_map/dot_general | solution.py:104
  223.2 0.0 copy-start.1
  223.2 0.0 reduce-scatter.5.cloned.1.call-update
  223.2 1.5 collective-permute-start.2
  224.7 0.0 copy-done.1
  224.8 0.0 copy-start.4
  224.8 0.1 constant_dynamic-slice_fusion.1
  224.9 1.5 collective-permute-start.1
  226.4 0.0 copy-done.4
  226.5 0.1 fusion.11.table_ref
  226.6 100.3 %collective-permute-done.1 = bf16[512,1024]{0,1:T(8,128)(2,1)S(1)} collective-permute-done((bf16[512,1024]{0,1:T(8,128)(2,1)S(1)}, bf16[512,1024]{0,1:T(8,128)(2,1)S(1)}, u32[]{:S(2)}, u32[]{:S(2)}) %collective-permute-start.1) | collective-permute-done | bytes 1048608 | tf_op jit(solution)/shard_map/ppermute | solution.py:64
  326.9 0.2 maximum_bitcast_fusion.turned_ref
  327.1 0.0 reduce-scatter.5.cloned.1.call-done
  327.1 2.9 collective-permute-start
  330.0 0.0 collective-permute-done.2.other_ref
  330.0 0.0 copy-start
  330.1 2.0 copy-done
  332.1 13.2 %rotated_grad.1 = f32[1024,3584]{1,0:T(8,128)} custom-call(bf16[1024,1024]{1,0:T(8,128)(2,1)S(1)} %maximum_bitcast_fusion.turned_ref, bf16[512,3584]{1,0:T(8,128)(2,1)S(1)} %copy-done, bf16[512,3584]{1,0:T(8,128)(2,1)} %collective-permute-done.2.other_ref, bf16[1,3584]{1,0:T(2,128)(2,1)S(1)} %broadcast_in_dim.2.sign_ref, bf16[128,128]{1,0:T(8,128)(2,1)S(1)} %fusion.11.table_ref), custom_call_target="tpu_custom_call" | custom-call | flops 7516192768 | bytes 22020096 | tf_op jit(solution)/shard_map/rotated_grad/pallas_call | solution.py:42
  345.3 8.2 %collective-permute-done = bf16[128,2048]{1,0:T(8,128)(2,1)S(1)} collective-permute-done((bf16[128,2048]{1,0:T(8,128)(2,1)}, bf16[128,2048]{1,0:T(8,128)(2,1)S(1)}, u32[]{:S(2)}, u32[]{:S(2)}) %collective-permute-start) | collective-permute-done | bytes 524320 | tf_op jit(solution)/shard_map/ppermute | solution.py:110
  353.5 0.8 copy.14
  (3 shorter events, 0.1 us)
Async XLA Ops:
  7.2 44.2 %all-gather.3.cloned.1.call-start = ((), (), s32[]{:S(2)}) async-start(), calls=%async_computation.3 | async-start | bytes 2621440 | tf_op jit(solution)/shard_map/all_gather | solution.py:85
  10.4 20.3 %copy-start.3 = (f32[16,3584]{1,0:T(8,128)S(1)}, f32[16,3584]{1,0:T(8,128)}, u32[]{:S(2)}) copy-start(f32[16,3584]{1,0:T(8,128)} %param.7) | copy-start | bytes 688132
  30.7 103.6 %reduce-scatter.3.cloned.1.call-start = ((), (), s32[]{:S(2)}) async-start(), calls=%async_computation.4 | async-start | bytes 4587520 | tf_op jit(solution)/shard_map/reduce_scatter | solution.py:91
  64.4 69.9 %copy-start.2 = (bf16[128,3584]{1,0:T(8,128)(2,1)S(1)}, bf16[128,3584]{1,0:T(8,128)(2,1)}, u32[]{:S(2)}) copy-start(bf16[128,3584]{1,0:T(8,128)(2,1)} %param.8) | copy-start | bytes 2752516
  64.4 145.6 %all-gather.5.cloned.1.call-start = ((), (), s32[]{:S(2)}) async-start(), calls=%async_computation.5 | async-start | bytes 4587520 | tf_op jit(solution)/shard_map/all_gather | solution.py:102
  137.6 189.6 %reduce-scatter.5.cloned.1.call-start = ((), (), s32[]{:S(2)}) async-start(), calls=%async_computation.6 | async-start | bytes 2621440 | tf_op jit(solution)/shard_map/reduce_scatter | solution.py:108
  223.2 1.6 copy-start.1
  223.2 106.8 %collective-permute-start.2 = (bf16[512,3584]{1,0:T(8,128)(2,1)}, bf16[512,3584]{1,0:T(8,128)(2,1)}, u32[]{:S(2)}, u32[]{:S(2)}) collective-permute-start(bf16[512,3584]{1,0:T(8,128)(2,1)} %all-gather.5.cloned.1.call-done.mine_ref), channel_id=1, source_target_pairs={{0,4},{4,0},{1,5},{5,1},{2,6},{6,2},{3,7},{7,3},{8,12},{12,8},{9,1... | collective-permute-start | bytes 11010056 | tf_op jit(solution)/shard_map/ppermute | solution.py:64
  224.8 1.7 copy-start.4
  224.9 102.0 %collective-permute-start.1 = (bf16[512,1024]{0,1:T(8,128)(2,1)S(1)}, bf16[512,1024]{0,1:T(8,128)(2,1)S(1)}, u32[]{:S(2)}, u32[]{:S(2)}) collective-permute-start(bf16[512,1024]{0,1:T(8,128)(2,1)S(1)} %get-tuple-element.4), channel_id=1, source_target_pairs={{0,4},{4,0},{1,5},{5,1},{2,6},{6,2},{3,7},{7,3},{8,12},{12,8},{9,1... | collective-permute-start | bytes 3145736 | tf_op jit(solution)/shard_map/ppermute | solution.py:64
  327.1 26.3 %collective-permute-start = (bf16[128,2048]{1,0:T(8,128)(2,1)}, bf16[128,2048]{1,0:T(8,128)(2,1)S(1)}, u32[]{:S(2)}, u32[]{:S(2)}) collective-permute-start(bf16[128,2048]{1,0:T(8,128)(2,1)} %reduce-scatter.5.cloned.1.call-done), channel_id=1, source_target_pairs={{0,0},{1,8},{2,16},{3,24},{8,1},{9,9},{10,17},{11,25},{16,2},{17,1... | collective-permute-start | bytes 1572872 | tf_op jit(solution)/shard_map/ppermute | solution.py:110
  330.0 2.0 copy-start
Sparse Core Ops, SparseCore 0:
  30.8 20.4 all-gather.2
  64.5 69.6 reduce-scatter.2
  137.7 72.3 all-gather.4
  223.3 28.6 reduce-scatter.4

commit v2 on v1

--- a/solution.py
+++ b/solution.py
@@ -60,6 +60,214 @@
     )(turned, mine, other, signs, hadamard_table(HB))
 
 
+MESH = pl.DeviceIdType.MESH
+
+
+def line_kernel(
+    n, width, part_ref, cot_ref, act_ref, mine_ref, other_ref,
+    sums, from_left, from_right, total,
+    sum_sent, left_came, right_came, up_sent, down_sent, came, cross_sent, cross_came,
+):
+    me = lax.axis_index("fsdp")
+    partner_id = 1 - lax.axis_index("replica")
+    high = jnp.minimum(me + 1, n - 1)
+    low = jnp.maximum(me - 1, 0)
+    rows = cot_ref.shape[0]
+    blocks = cot_ref.shape[1] // width
+    has_low, has_high = me > 0, me < n - 1
+
+    def at(ref, owner, c):
+        start = owner * rows if isinstance(owner, int) else pl.multiple_of(owner * rows, rows)
+        return ref.at[pl.ds(start, rows), pl.ds(pl.multiple_of(c * width, width), width)]
+
+    def move(source, target, owner, c, send, recv, device):
+        return pltpu.make_async_remote_copy(
+            src_ref=at(source, owner, c), dst_ref=at(target, owner, c),
+            send_sem=send.at[owner, c], recv_sem=recv.at[owner, c],
+            device_id=device, device_id_type=MESH,
+        )
+
+    def sum_up(d, c):
+        return move(sums, from_left, d, c, sum_sent, left_came, {"fsdp": high})
+
+    def sum_down(d, c):
+        return move(sums, from_right, d, c, sum_sent, right_came, {"fsdp": low})
+
+    def go_up(s, c):
+        return move(mine_ref, mine_ref, s, c, up_sent, came, {"fsdp": high})
+
+    def go_down(s, c):
+        return move(mine_ref, mine_ref, s, c, down_sent, came, {"fsdp": low})
+
+    def cross(s, c):
+        return move(mine_ref, other_ref, s, c, cross_sent, cross_came, {"replica": partner_id})
+
+    def within(c):
+        return jnp.logical_and(c >= 0, c < blocks)
+
+    barrier = pltpu.get_barrier_semaphore()
+    pl.semaphore_signal(barrier, inc=1, device_id={"replica": partner_id}, device_id_type=MESH)
+
+    @pl.when(has_low)
+    def _():
+        pl.semaphore_signal(barrier, inc=1, device_id={"fsdp": low}, device_id_type=MESH)
+
+    @pl.when(has_high)
+    def _():
+        pl.semaphore_signal(barrier, inc=1, device_id={"fsdp": high}, device_id_type=MESH)
+
+    pl.semaphore_wait(barrier, 1 + jnp.where(has_low, 1, 0) + jnp.where(has_high, 1, 0))
+
+    def reduce_chain(c, first, owners, applies, arrival, send):
+        @pl.when(within(c))
+        def _():
+            for d in owners:
+                @pl.when(applies(d))
+                def _():
+                    @pl.when(first)
+                    def _():
+                        at(sums, d, c)[...] = at(part_ref, d, c)[...]
+
+                    @pl.when(jnp.logical_not(first))
+                    def _():
+                        arrival[1](d, c).wait_recv()
+                        at(sums, d, c)[...] = (
+                            at(part_ref, d, c)[...].astype(jnp.float32)
+                            + at(arrival[0], d, c)[...].astype(jnp.float32)
+                        ).astype(jnp.bfloat16)
+            for d in owners:
+                @pl.when(applies(d))
+                def _():
+                    send(d, c).start()
+
+    def step(i, carry):
+        reduce_chain(
+            i - me, me == 0, range(n - 1, 0, -1), lambda d: me < d, (from_left, sum_up), sum_up
+        )
+        reduce_chain(
+            i - (n - 1 - me), me == n - 1, range(n - 1), lambda d: me > d, (from_right, sum_down), sum_down
+        )
+        c = i - (n - 1)
+
+        @pl.when(within(c))
+        def _():
+            total[...] = at(part_ref, me, c)[...].astype(jnp.float32)
+
+            @pl.when(has_low)
+            def _():
+                sum_up(me, c).wait_recv()
+                total[...] += at(from_left, me, c)[...].astype(jnp.float32)
+
+            @pl.when(has_high)
+            def _():
+                sum_down(me, c).wait_recv()
+                total[...] += at(from_right, me, c)[...].astype(jnp.float32)
+
+            hidden = total[...]
+            sig = jax.nn.sigmoid(hidden)
+            at(act_ref, 0, c)[...] = (hidden * sig).astype(jnp.bfloat16)
+            at(mine_ref, me, c)[...] = (
+                at(cot_ref, 0, c)[...].astype(jnp.float32) * sig * (1.0 + hidden * (1.0 - sig))
+            ).astype(jnp.bfloat16)
+
+            @pl.when(has_high)
+            def _():
+                go_up(me, c).start()
+
+            @pl.when(has_low)
+            def _():
+                go_down(me, c).start()
+
+            cross(me, c).start()
+
+        for k in range(1, n):
+            late = i - (n - 1 + k)
+
+            @pl.when(jnp.logical_and(within(late), me - k >= 0))
+            def _():
+                s = me - k
+                go_up(s, late).wait_recv()
+
+                @pl.when(has_high)
+                def _():
+                    go_up(s, late).start()
+
+                cross(s, late).start()
+
+            @pl.when(jnp.logical_and(within(late), me + k < n))
+            def _():
+                s = me + k
+                go_down(s, late).wait_recv()
+
+                @pl.when(has_low)
+                def _():
+                    go_down(s, late).start()
+
+                cross(s, late).start()
+
+        return carry
+
+    lax.fori_loop(0, blocks + 2 * (n - 1), step, 0)
+
+    def drain(c, carry):
+        for d in range(n):
+            @pl.when(me != d)
+            def _():
+                sum_up(d, c).wait_send()
+
+            @pl.when(jnp.logical_and(has_high, me >= d))
+            def _():
+                go_up(d, c).wait_send()
+
+            @pl.when(jnp.logical_and(has_low, me <= d))
+            def _():
+                go_down(d, c).wait_send()
+
+            cross(d, c).wait_send()
+            cross(d, c).wait_recv()
+        return carry
+
+    lax.fori_loop(0, blocks, drain, 0)
+
+
+def line_exchange(partial, cotangent, n):
+    rows, cols = partial.shape
+    width = next(t for t in (512, 256, HB) if cols % t == 0)
+    vmem = pl.BlockSpec(memory_space=pltpu.VMEM)
+    whole = jax.ShapeDtypeStruct((rows, cols), jnp.bfloat16)
+    sems = pltpu.SemaphoreType.DMA((n, cols // width))
+    return pl.pallas_call(
+        functools.partial(line_kernel, n, width),
+        out_shape=(jax.ShapeDtypeStruct(cotangent.shape, jnp.bfloat16), whole, whole),
+        in_specs=[vmem, vmem],
+        out_specs=(vmem, vmem, vmem),
+        scratch_shapes=[pltpu.VMEM((rows, cols), jnp.bfloat16)] * 3
+        + [pltpu.VMEM((rows // n, width), jnp.float32)]
+        + [sems] * 8,
+        compiler_params=pltpu.CompilerParams(
+            collective_id=0, has_side_effects=True, vmem_limit_bytes=60 * 1024 * 1024
+        ),
+        name="line_exchange",
+    )(partial, cotangent)
+
+
+def halve(array, keep, n_tensor, bit):
+    lead = lax.dynamic_index_in_dim(array, keep, 0, keepdims=False)
+    sent = lax.dynamic_index_in_dim(array, 1 - keep, 0, keepdims=False)
+    came = lax.ppermute(sent, "tensor", [(t, t ^ bit) for t in range(n_tensor)])
+    return (lead.astype(jnp.float32) + came.astype(jnp.float32)).astype(jnp.bfloat16)
+
+
+def tensor_reduce(product, n_tensor):
+    if n_tensor != 4:
+        return lax.psum_scatter(product, "tensor", scatter_dimension=0, tiled=True)
+    rows, cols = product.shape
+    place = lax.axis_index("tensor")
+    chunks = product.reshape(2, 2, rows // 4, cols).swapaxes(0, 1)
+    chunks = halve(chunks, place % 2, n_tensor, 1)
+    return halve(chunks, place // 2, n_tensor, 2)
+
+
 def partner(array):
     return lax.ppermute(array, "replica", [(0, 1), (1, 0)])
 
@@ -88,24 +296,23 @@
     kept = lax.dynamic_slice_in_dim(columns, replica * half_rows, half_rows, 1)
     sent = lax.dynamic_slice_in_dim(columns, (1 - replica) * half_rows, half_rows, 1)
     turned = jnp.concatenate([kept, partner(sent)], axis=0).T
-    hidden = lax.psum_scatter(
-        jnp.dot(columns, weight, preferred_element_type=jnp.float32).astype(jnp.bfloat16),
-        "fsdp",
-        scatter_dimension=0,
-        tiled=True,
-    ).astype(jnp.float32)
-    sigmoid_val = jax.nn.sigmoid(hidden)
-    activation = (hidden * sigmoid_val).astype(jnp.bfloat16)
-    hidden_grad = (
-        cotangent.astype(jnp.float32) * sigmoid_val * (1.0 + hidden * (1.0 - sigmoid_val))
-    ).astype(jnp.bfloat16)
-    arrived = lax.all_gather(hidden_grad, "fsdp", axis=0, tiled=True)
-    other = partner(arrived)
+    partial = jnp.dot(columns, weight, preferred_element_type=jnp.float32).astype(jnp.bfloat16)
+    if n_fsdp > 1 and 12 * partial.size <= 40 * 1024 * 1024:
+        activation, arrived, other = line_exchange(partial, cotangent, n_fsdp)
+    else:
+        hidden = lax.psum_scatter(partial, "fsdp", scatter_dimension=0, tiled=True).astype(jnp.float32)
+        sigmoid_val = jax.nn.sigmoid(hidden)
+        activation = (hidden * sigmoid_val).astype(jnp.bfloat16)
+        hidden_grad = (
+            cotangent.astype(jnp.float32) * sigmoid_val * (1.0 + hidden * (1.0 - sigmoid_val))
+        ).astype(jnp.bfloat16)
+        arrived = lax.all_gather(hidden_grad, "fsdp", axis=0, tiled=True)
+        other = partner(arrived)
     product = lax.dot_general(
         arrived, weight, (((1,), (1,)), ((), ())), preferred_element_type=jnp.float32
     ).astype(jnp.bfloat16)
     if n_fsdp == n_tensor:
-        summed = lax.psum_scatter(product, "tensor", scatter_dimension=0, tiled=True)
+        summed = tensor_reduce(product, n_tensor)
         swap = [(f * n_tensor + t, t * n_tensor + f) for f in range(n_fsdp) for t in range(n_tensor)]
         input_grad = lax.ppermute(summed, ("fsdp", "tensor"), swap)
     else:

time: 361 us -> 268 us (0.74)
  waiting for transfers between devices: 257 us -> 38.2 us
  Pallas kernels: 13.2 us -> 135 us
    pallas_call x0 -> x1, Pallas kernels: none -> 121 us  [line_exchange(): pl.pallas_call(functools.partial(line_kernel, n, width), out_shape=(jax.S...]
    ppermute x2 -> x1, waiting for transfers between devices: 100 us -> 19.9 us  [partner(): return lax.ppermute(array, 'replica', [(0, 1), (1, 0)])]
    all_gather x1 -> x0, waiting for transfers between devices: 72.4 us -> none  [shards(): arrived = lax.all_gather(hidden_grad, 'fsdp', axis=0, tiled=True)]
    reduce_scatter x2 -> x0, waiting for transfers between devices: 69.8 us -> none  [the longest x1 69.8 us: shards(): lax.psum_scatter(jnp.dot(columns, weight, preferred_element_type=jnp.floa...]
  transfers between devices with their start and end apart: 7 -> 5, of which waited for: 5 -> 4; matrix products, arithmetic and copies ran while one was open for 4% -> 7% of each run, Pallas kernels for 4% -> 5%
where the time goes in v2:
time: 268 us; the launch traced here: 267 us
  Pallas kernels  135 us (50%)
  waiting for transfers between devices  38.2 us (14%)
  matrix products  25.3 us (9%)
  blocking collectives  19.2 us (7%)
  other arithmetic  17.5 us (7%)
  between operations  14.2 us (5%)
  local copies, waits for them, and re-layouts  10.3 us (4%)
  starting transfers between devices  8.01 us (3%)
    pallas_call x1, Pallas kernels, line_exchange(): pl.pallas_call(functools.partial(line_kernel, n, width), out_shape=(jax.S...  121 us
    ppermute x1, waiting for transfers between devices, partner(): return lax.ppermute(array, 'replica', [(0, 1), (1, 0)])  19.9 us
    all_to_all x1, blocking collectives, shards(): lax.all_to_all(own, 'fsdp', split_axis=1, concat_axis=0, tiled=True)  19.2 us
    convert_element_type x1, other arithmetic, shards(): weight = (weight_codes.astype(jnp.float32).reshape(scales.shape[0], block...  14.1 us
    pallas_call x1, Pallas kernels, rotated_grad(): pl.pallas_call(functools.partial(grad_kernel, scaling), grid=(width // ti...  13.3 us
    dot_general x1, matrix products, shards(): jnp.dot(columns, weight, preferred_element_type=jnp.float32)  13 us
    dot_general x1, matrix products, shards(): lax.dot_general(arrived, weight, (((1,), (1,)), ((), ())), preferred_elem...  12.3 us
    ppermute x1, waiting for transfers between devices, shards(): input_grad = lax.ppermute(summed, ('fsdp', 'tensor'), swap)  10.5 us
  transfers between devices with their start and end apart: 5, of which 4 were waited for; matrix products, arithmetic and copies ran while one was open for 7% of the time, Pallas kernels for 5%

profile of v2, /device:TPU:4, one launch (start us, length us, event | category | flops | bytes accessed | tf_op | source)
XLA Modules:
  0.0 267.4 jit_solution(46212686714942073)
XLA Ops:
  7.2 0.0 all-gather.2.cloned.1.call-start
  7.2 0.0 copy-start.5
  7.2 3.3 %copy.10 = bf16[128,8192]{0,1:T(8,128)(2,1)S(1)} copy(bf16[128,8192]{1,0:T(8,128)(2,1)} %param.5) | data formatting | bytes 4194304 | tf_op args[0]
  10.6 19.2 %all_to_all.16 = bf16[128,4,512]{0,2,1:T(8,128)(2,1)S(1)} all-to-all(bf16[128,4,512]{0,2,1:T(8,128)(2,1)S(1)} %constant_dynamic-slice_fusion.2), channel_id=1, replica_groups=mesh['fsdp'=4,'replica'=2,'tensor'=4] {'fsdp'}, dimensions={1} | all-to-all | bytes 1048576 | tf_op jit(solution)/shard_map/all_to_all | solution.py:292
  29.7 0.9 copy_bitcast_fusion
  30.6 0.0 all-gather.2.cloned.1.call-update
  30.6 0.0 copy-done.5
  30.6 14.1 %fusion = bf16[2048,3584]{1,0:T(8,128)(2,1)} fusion(bf16[2048,3584]{1,0:T(8,128)(2,1)} %param.6, f32[16,3584]{1,0:T(8,128)S(1)} %copy-done.5), kind=kLoop, calls=%fused_computation.1 | loop fusion | flops 22020096 | bytes 29589504 | tf_op jit(solution)/shard_map/convert_element_type | solution.py:286
  44.8 6.5 %all-gather.2.cloned.1.call-done = bf16[512,2048]{0,1:T(8,128)(2,1)} async-done(((bf16[512,512]{0,1:T(8,128)(2,1)}), bf16[512,2048]{0,1:T(8,128)(2,1)}) %all-gather.2.cloned.1.call-update) | async-done | bytes 2097168 | tf_op jit(solution)/shard_map/all_gather | solution.py:293
  51.2 13.0 %convolution_convert_fusion.part_ref = bf16[512,3584]{1,0:T(8,128)(2,1)} fusion(bf16[512,2048]{0,1:T(8,128)(2,1)} %all-gather.2.cloned.1.call-done, bf16[2048,3584]{1,0:T(8,128)(2,1)} %fusion), kind=kOutput, calls=%fused_computation.2 | convolution fusion | flops 7518027776 | bytes 20447232 | tf_op jit(solution)/shard_map/dot_general | solution.py:299
  64.3 121.4 %line_exchange.1 = (bf16[128,3584]{1,0:T(8,128)(2,1)}, bf16[512,3584]{1,0:T(8,128)(2,1)}, bf16[512,3584]{1,0:T(8,128)(2,1)}) custom-call(bf16[512,3584]{1,0:T(8,128)(2,1)} %convolution_convert_fusion.part_ref, bf16[128,3584]{1,0:T(8,128)(2,1)} %cot_ref.1), custom_call_target="tpu_custom_call" | custom-call | tf_op jit(solution)/shard_map/line_exchange/pallas_call | solution.py:239
  185.7 0.0 copy-start.1
  185.7 12.3 %convolution_convert_fusion.1 = bf16[512,2048]{1,0:T(8,128)(2,1)S(1)} fusion(bf16[512,3584]{1,0:T(8,128)(2,1)} %get-tuple-element.7.mine_ref, bf16[2048,3584]{1,0:T(8,128)(2,1)} %fusion), kind=kOutput, calls=%fused_computation.3 | convolution fusion | flops 7517241344 | bytes 20447232 | tf_op jit(solution)/shard_map/dot_general | solution.py:311
  198.0 0.0 copy-start.2
  198.0 1.3 copy-done.2
  199.3 1.1 dynamic-slice_bitcast_fusion
  200.4 0.0 collective-permute-start
  200.4 0.0 copy-done.1
  200.4 0.0 copy-start.3
  200.4 0.0 copy-start.6
  200.4 1.1 constant_dynamic-slice_fusion.1
  201.5 0.6 collective-permute-start.3
  202.1 1.3 collective-permute-done
  203.4 0.0 copy-done.3
  203.4 1.6 fusion.1
  205.0 0.8 dynamic-slice_bitcast_fusion.1
  205.9 1.5 collective-permute-start.1
  207.4 0.0 copy-done.6
  207.4 0.0 copy-start
  207.4 0.1 fusion.6.table_ref
  207.5 19.9 %collective-permute-done.3 = bf16[512,1024]{0,1:T(8,128)(2,1)} collective-permute-done((bf16[512,1024]{0,1:T(8,128)(2,1)}, bf16[512,1024]{0,1:T(8,128)(2,1)}, u32[]{:S(2)}, u32[]{:S(2)}) %collective-permute-start.3) | collective-permute-done | bytes 1048608 | tf_op jit(solution)/shard_map/ppermute | solution.py:272
  227.4 1.5 maximum_bitcast_fusion.turned_ref
  228.9 0.0 collective-permute-done.1
  228.9 0.1 fusion.2
  229.1 5.9 %collective-permute-start.2 = (bf16[128,2048]{1,0:T(8,128)(2,1)S(1)}, bf16[128,2048]{1,0:T(8,128)(2,1)S(1)}, u32[]{:S(2)}, u32[]{:S(2)}) collective-permute-start(bf16[128,2048]{1,0:T(8,128)(2,1)S(1)} %fusion.2), channel_id=1, source_target_pairs={{0,0},{1,8},{2,16},{3,24},{8,1},{9,9},{10,17},{11,25},{16,2},{17,1... | collective-permute-start | bytes 1572872 | tf_op jit(solution)/shard_map/ppermute | solution.py:317
  235.0 0.0 copy-done
  235.0 0.0 copy-start.4
  235.0 13.3 %rotated_grad.1 = f32[1024,3584]{1,0:T(8,128)} custom-call(bf16[1024,1024]{1,0:T(8,128)(2,1)S(1)} %maximum_bitcast_fusion.turned_ref, bf16[512,3584]{1,0:T(8,128)(2,1)S(1)} %copy-done, bf16[512,3584]{1,0:T(8,128)(2,1)} %get-tuple-element.8.other_ref, bf16[1,3584]{1,0:T(2,128)(2,1)S(1)} %broadcast_in_dim.2.sign_ref, bf16[128,128]{1,0:T(8,128)(2,1)S(1)} %fusion.6.table_ref), custom_call_target="tpu_custom_call" | custom-call | flops 7516192768 | bytes 22020096 | tf_op jit(solution)/shard_map/rotated_grad/pallas_call | solution.py:42
  248.3 10.5 %collective-permute-done.2 = bf16[128,2048]{1,0:T(8,128)(2,1)S(1)} collective-permute-done((bf16[128,2048]{1,0:T(8,128)(2,1)S(1)}, bf16[128,2048]{1,0:T(8,128)(2,1)S(1)}, u32[]{:S(2)}, u32[]{:S(2)}) %collective-permute-start.2) | collective-permute-done | bytes 524320 | tf_op jit(solution)/shard_map/ppermute | solution.py:317
  258.8 0.0 copy-done.4
  258.8 0.9 copy.18
  259.8 0.8 copy.19
  (3 shorter events, 0.1 us)
Async XLA Ops:
  7.2 44.1 %all-gather.2.cloned.1.call-start = ((), (), s32[]{:S(2)}) async-start(), calls=%async_computation.1 | async-start | bytes 2621440 | tf_op jit(solution)/shard_map/all_gather | solution.py:293
  7.2 23.4 %copy-start.5 = (f32[16,3584]{1,0:T(8,128)S(1)}, f32[16,3584]{1,0:T(8,128)}, u32[]{:S(2)}) copy-start(f32[16,3584]{1,0:T(8,128)} %param.7) | copy-start | bytes 688132
  185.7 14.7 %copy-start.1 = (bf16[512,2048]{0,1:T(8,128)(2,1)S(1)}, bf16[512,2048]{0,1:T(8,128)(2,1)}, u32[]{:S(2)}) copy-start(bf16[512,2048]{0,1:T(8,128)(2,1)} %all-gather.2.cloned.1.call-done) | copy-start | bytes 6291460
  198.0 1.3 copy-start.2
  200.4 3.0 %collective-permute-start = (bf16[2,128,2048]{2,1,0:T(8,128)(2,1)}, bf16[2,128,2048]{2,1,0:T(8,128)(2,1)}, u32[]{:S(2)}, u32[]{:S(2)}) collective-permute-start(bf16[2,128,2048]{2,1,0:T(8,128)(2,1)} %dynamic-slice_bitcast_fusion), channel_id=1, source_target_pairs={{0,1},{1,0},{2,3},{3,2},{4,5},{5,4},{6,7},{7,6},{8,9},{9,8},{10,11... | collective-permute-start | bytes 3145736 | tf_op jit(solution)/shard_map/ppermute | solution.py:257
  200.4 3.0 %copy-start.3 = (bf16[512,2048]{1,0:T(8,128)(2,1)S(1)}, bf16[512,2048]{1,0:T(8,128)(2,1)}, u32[]{:S(2)}) copy-start(bf16[512,2048]{1,0:T(8,128)(2,1)} %copy-done.2) | copy-start | bytes 6291460
  200.4 6.9 %copy-start.6 = (s32[3584]{0:T(1024)S(1)}, s32[3584]{0:T(1024)}, u32[]{:S(2)}) copy-start(s32[3584]{0:T(1024)} %param.9) | copy-start | bytes 43012
  201.5 25.9 %collective-permute-start.3 = (bf16[512,1024]{0,1:T(8,128)(2,1)}, bf16[512,1024]{0,1:T(8,128)(2,1)}, u32[]{:S(2)}, u32[]{:S(2)}) collective-permute-start(bf16[512,1024]{0,1:T(8,128)(2,1)} %get-tuple-element.10), channel_id=1, source_target_pairs={{0,4},{4,0},{1,5},{5,1},{2,6},{6,2},{3,7},{7,3},{8,12},{12,8},{9,1... | collective-permute-start | bytes 3145736 | tf_op jit(solution)/shard_map/ppermute | solution.py:272
  205.9 23.0 %collective-permute-start.1 = (bf16[128,2048]{1,0:T(8,128)(2,1)}, bf16[128,2048]{1,0:T(8,128)(2,1)S(1)}, u32[]{:S(2)}, u32[]{:S(2)}) collective-permute-start(bf16[128,2048]{1,0:T(8,128)(2,1)} %dynamic-slice_bitcast_fusion.1), channel_id=1, source_target_pairs={{0,2},{1,3},{2,0},{3,1},{4,6},{5,7},{6,4},{7,5},{8,10},{9,11},{10,... | collective-permute-start | bytes 1572872 | tf_op jit(solution)/shard_map/ppermute | solution.py:257
  207.4 27.6 %copy-start = (bf16[512,3584]{1,0:T(8,128)(2,1)S(1)}, bf16[512,3584]{1,0:T(8,128)(2,1)}, u32[]{:S(2)}) copy-start(bf16[512,3584]{1,0:T(8,128)(2,1)} %get-tuple-element.7.mine_ref) | copy-start | bytes 11010052
  229.1 29.8 %collective-permute-start.2 = (bf16[128,2048]{1,0:T(8,128)(2,1)S(1)}, bf16[128,2048]{1,0:T(8,128)(2,1)S(1)}, u32[]{:S(2)}, u32[]{:S(2)}) collective-permute-start(bf16[128,2048]{1,0:T(8,128)(2,1)S(1)} %fusion.2), channel_id=1, source_target_pairs={{0,0},{1,8},{2,16},{3,24},{8,1},{9,9},{10,17},{11,25},{16,2},{17,1... | collective-permute-start | bytes 1572872 | tf_op jit(solution)/shard_map/ppermute | solution.py:317
  235.0 23.8 %copy-start.4 = (bf16[128,3584]{1,0:T(8,128)(2,1)S(1)}, bf16[128,3584]{1,0:T(8,128)(2,1)}, u32[]{:S(2)}) copy-start(bf16[128,3584]{1,0:T(8,128)(2,1)} %get-tuple-element.14) | copy-start | bytes 2752516
Sparse Core Ops, SparseCore 0:
  30.7 20.4 all-gather.1

commit v3 on v2

--- a/solution.py
+++ b/solution.py
@@ -64,8 +64,8 @@
 
 
 def line_kernel(
-    n, width, part_ref, cot_ref, act_ref, mine_ref, other_ref,
-    sums, from_left, from_right, total,
+    n, width, tokens_ref, weight_hbm, cot_ref, act_ref, mine_ref, other_ref, product_ref, across_ref,
+    part_ref, sums, from_left, from_right, total, weight_ref, gathered, fetched, swap_sent, swap_came,
     sum_sent, left_came, right_came, up_sent, down_sent, came, cross_sent, cross_came,
 ):
     me = lax.axis_index("fsdp")
@@ -105,6 +105,23 @@
     def within(c):
         return jnp.logical_and(c >= 0, c < blocks)
 
+    def fetch(c):
+        cols = pl.ds(pl.multiple_of(c * width, width), width)
+        return pltpu.make_async_copy(weight_hbm.at[:, cols], weight_ref.at[:, cols], fetched.at[c])
+
+    def fetch_all(c, carry):
+        fetch(c).start()
+        return carry
+
+    lax.fori_loop(0, blocks, fetch_all, 0)
+
+    def project(c):
+        fetch(c).wait()
+        cols = pl.ds(pl.multiple_of(c * width, width), width)
+        part_ref[:, cols] = jnp.dot(
+            tokens_ref[...], weight_ref[:, cols], preferred_element_type=jnp.float32
+        ).astype(jnp.bfloat16)
+
     barrier = pltpu.get_barrier_semaphore()
     pl.semaphore_signal(barrier, inc=1, device_id={"replica": partner_id}, device_id_type=MESH)
 
@@ -117,6 +134,16 @@
         pl.semaphore_signal(barrier, inc=1, device_id={"fsdp": high}, device_id_type=MESH)
 
     pl.semaphore_wait(barrier, 1 + jnp.where(has_low, 1, 0) + jnp.where(has_high, 1, 0))
+
+    depth = across_ref.shape[1]
+    swap = pltpu.make_async_remote_copy(
+        src_ref=tokens_ref.at[:, pl.ds(pl.multiple_of(partner_id * depth, depth), depth)],
+        dst_ref=across_ref, send_sem=swap_sent, recv_sem=swap_came,
+        device_id={"replica": partner_id}, device_id_type=MESH,
+    )
+    swap.start()
+    gathered[...] = jnp.zeros_like(gathered)
+    project(0)
 
     def reduce_chain(c, first, owners, applies, arrival, send):
         @pl.when(within(c))
@@ -205,9 +232,26 @@
 
                 cross(s, late).start()
 
+        @pl.when(i + 1 < blocks)
+        def _():
+            project(i + 1)
+
+        done = i - 2 * (n - 1)
+
+        @pl.when(done >= 0)
+        def _():
+            cols = pl.ds(pl.multiple_of(done * width, width), width)
+            gathered[...] += lax.dot_general(
+                mine_ref[:, cols], weight_ref[:, cols], (((1,), (1,)), ((), ())),
+                preferred_element_type=jnp.float32,
+            )
+
         return carry
 
     lax.fori_loop(0, blocks + 2 * (n - 1), step, 0)
+
+    product_ref[...] = gathered[...].astype(jnp.bfloat16)
+    swap.wait()
 
     def drain(c, carry):
         for d in range(n):
@@ -230,25 +274,39 @@
     lax.fori_loop(0, blocks, drain, 0)
 
 
-def line_exchange(partial, cotangent, n):
-    rows, cols = partial.shape
-    width = next(t for t in (512, 256, HB) if cols % t == 0)
+def line_exchange(columns, weight, cotangent, n):
+    rows, depth = columns.shape
+    cols = weight.shape[1]
+    width = next(t for t in (256, HB) if cols % t == 0)
     vmem = pl.BlockSpec(memory_space=pltpu.VMEM)
     whole = jax.ShapeDtypeStruct((rows, cols), jnp.bfloat16)
     sems = pltpu.SemaphoreType.DMA((n, cols // width))
     return pl.pallas_call(
         functools.partial(line_kernel, n, width),
-        out_shape=(jax.ShapeDtypeStruct(cotangent.shape, jnp.bfloat16), whole, whole),
-        in_specs=[vmem, vmem],
-        out_specs=(vmem, vmem, vmem),
-        scratch_shapes=[pltpu.VMEM((rows, cols), jnp.bfloat16)] * 3
-        + [pltpu.VMEM((rows // n, width), jnp.float32)]
+        out_shape=(
+            jax.ShapeDtypeStruct(cotangent.shape, jnp.bfloat16),
+            whole,
+            whole,
+            jax.ShapeDtypeStruct((rows, depth), jnp.bfloat16),
+            jax.ShapeDtypeStruct((rows, depth // 2), jnp.bfloat16),
+        ),
+        in_specs=[vmem, pl.BlockSpec(memory_space=pl.ANY), vmem],
+        out_specs=(vmem,) * 5,
+        scratch_shapes=[pltpu.VMEM((rows, cols), jnp.bfloat16)] * 4
+        + [
+            pltpu.VMEM((rows // n, width), jnp.float32),
+            pltpu.VMEM(weight.shape, jnp.bfloat16),
+            pltpu.VMEM((rows, depth), jnp.float32),
+            pltpu.SemaphoreType.DMA((cols // width,)),
+            pltpu.SemaphoreType.DMA,
+            pltpu.SemaphoreType.DMA,
+        ]
         + [sems] * 8,
         compiler_params=pltpu.CompilerParams(
             collective_id=0, has_side_effects=True, vmem_limit_bytes=60 * 1024 * 1024
         ),
         name="line_exchange",
-    )(partial, cotangent)
+    )(columns, weight, cotangent)
 
 
 def halve(array, keep, n_tensor, bit):
@@ -294,13 +352,18 @@
     half_rows = shard_rows // 2
     replica = lax.axis_index("replica")
     kept = lax.dynamic_slice_in_dim(columns, replica * half_rows, half_rows, 1)
-    sent = lax.dynamic_slice_in_dim(columns, (1 - replica) * half_rows, half_rows, 1)
-    turned = jnp.concatenate([kept, partner(sent)], axis=0).T
-    partial = jnp.dot(columns, weight, preferred_element_type=jnp.float32).astype(jnp.bfloat16)
-    if n_fsdp > 1 and 12 * partial.size <= 40 * 1024 * 1024:
-        activation, arrived, other = line_exchange(partial, cotangent, n_fsdp)
+    gathered = n_fsdp * local_tokens
+    held = 2 * shard_rows * hidden_cols + 12 * gathered * hidden_cols + 9 * gathered * shard_rows
+    if n_fsdp > 1 and held <= 52 * 1024 * 1024:
+        activation, arrived, other, product, across = line_exchange(columns, weight, cotangent, n_fsdp)
     else:
-        hidden = lax.psum_scatter(partial, "fsdp", scatter_dimension=0, tiled=True).astype(jnp.float32)
+        across = partner(lax.dynamic_slice_in_dim(columns, (1 - replica) * half_rows, half_rows, 1))
+        hidden = lax.psum_scatter(
+            jnp.dot(columns, weight, preferred_element_type=jnp.float32).astype(jnp.bfloat16),
+            "fsdp",
+            scatter_dimension=0,
+            tiled=True,
+        ).astype(jnp.float32)
         sigmoid_val = jax.nn.sigmoid(hidden)
         activation = (hidden * sigmoid_val).astype(jnp.bfloat16)
         hidden_grad = (
@@ -308,9 +371,10 @@
         ).astype(jnp.bfloat16)
         arrived = lax.all_gather(hidden_grad, "fsdp", axis=0, tiled=True)
         other = partner(arrived)
-    product = lax.dot_general(
-        arrived, weight, (((1,), (1,)), ((), ())), preferred_element_type=jnp.float32
-    ).astype(jnp.bfloat16)
+        product = lax.dot_general(
+            arrived, weight, (((1,), (1,)), ((), ())), preferred_element_type=jnp.float32
+        ).astype(jnp.bfloat16)
+    turned = jnp.concatenate([kept, across], axis=0).T
     if n_fsdp == n_tensor:
         summed = tensor_reduce(product, n_tensor)
         swap = [(f * n_tensor + t, t * n_tensor + f) for f in range(n_fsdp) for t in range(n_tensor)]

time: 268 us -> 231 us (0.86)
  matrix products: 25.3 us -> 0 us
  waiting for transfers between devices: 38.2 us -> 28.5 us
  Pallas kernels: 135 us -> 128 us
  local copies, waits for them, and re-layouts: 10.3 us -> 15.6 us
    dot_general x2 -> x0, matrix products: 25.3 us -> none  [the longest x1 13 us: shards(): jnp.dot(columns, weight, preferred_element_type=jnp.float32)]
    ppermute x1 -> x0, waiting for transfers between devices: 19.9 us -> none  [partner(): return lax.ppermute(array, 'replica', [(0, 1), (1, 0)])]
    ppermute x2, waiting for transfers between devices: 1.32 us -> 11.6 us  [halve(): came = lax.ppermute(sent, 'tensor', [(t, t ^ bit) for t in range(n_tensor)])]
    pallas_call x1, Pallas kernels: 121 us -> 115 us  [line_exchange(): pl.pallas_call(functools.partial(line_kernel, n, width), out_shape=(jax.S...]
    all_gather x0 -> x1, local copies, waits for them, and re-layouts: none -> 3.97 us  [shards(): columns = lax.all_gather(quarter, 'tensor', axis=1, tiled=True)]
  transfers between devices with their start and end apart: 5 -> 4, of which waited for: 4 -> 4; matrix products, arithmetic and copies ran while one was open for 7% -> 7% of each run, Pallas kernels for 5% -> 6%
where the time goes in v3:
time: 231 us; the launch traced here: 230 us
  Pallas kernels  128 us (55%)
  waiting for transfers between devices  28.5 us (12%)
  blocking collectives  19.3 us (8%)
  other arithmetic  17.3 us (7%)
  local copies, waits for them, and re-layouts  15.6 us (7%)
  between operations  14.2 us (6%)
  starting transfers between devices  6.83 us (3%)
    pallas_call x1, Pallas kernels, line_exchange(): pl.pallas_call(functools.partial(line_kernel, n, width), out_shape=(jax.S...  115 us
    all_to_all x1, blocking collectives, shards(): lax.all_to_all(own, 'fsdp', split_axis=1, concat_axis=0, tiled=True)  19.3 us
    convert_element_type x1, other arithmetic, shards(): weight = (weight_codes.astype(jnp.float32).reshape(scales.shape[0], block...  14.1 us
    pallas_call x1, Pallas kernels, rotated_grad(): pl.pallas_call(functools.partial(grad_kernel, scaling), grid=(width // ti...  13.3 us
    ppermute x2, waiting for transfers between devices, halve(): came = lax.ppermute(sent, 'tensor', [(t, t ^ bit) for t in range(n_tensor)])  11.6 us
    ppermute x1, waiting for transfers between devices, shards(): input_grad = lax.ppermute(summed, ('fsdp', 'tensor'), swap)  10.4 us
    all_gather x1, waiting for transfers between devices, shards(): columns = lax.all_gather(quarter, 'tensor', axis=1, tiled=True)  6.49 us
    unnamed x17, local copies, waits for them, and re-layouts  6.12 us
  transfers between devices with their start and end apart: 4, of which 4 were waited for; matrix products, arithmetic and copies ran while one was open for 7% of the time, Pallas kernels for 6%

profile of v3, /device:TPU:4, one launch (start us, length us, event | category | flops | bytes accessed | tf_op | source)
XLA Modules:
  0.0 230.2 jit_solution(5892412374475798751)
XLA Ops:
  7.2 0.0 all-gather.2.cloned.1.call-start
  7.2 3.2 %copy.12 = bf16[128,8192]{0,1:T(8,128)(2,1)S(1)} copy(bf16[128,8192]{1,0:T(8,128)(2,1)} %param.5) | data formatting | bytes 4194304 | tf_op args[0]
  10.4 0.0 copy-start.5
  10.5 19.3 %all_to_all.16 = bf16[128,4,512]{0,2,1:T(8,128)(2,1)S(1)} all-to-all(bf16[128,4,512]{0,2,1:T(8,128)(2,1)S(1)} %constant_dynamic-slice_fusion.1), channel_id=1, replica_groups=mesh['fsdp'=4,'replica'=2,'tensor'=4] {'fsdp'}, dimensions={1} | all-to-all | bytes 1048576 | tf_op jit(solution)/shard_map/all_to_all | solution.py:350
  29.8 0.9 copy_bitcast_fusion
  30.7 0.0 all-gather.2.cloned.1.call-update
  30.7 0.0 copy-done.5
  30.7 14.1 %fusion.weight_hbm = bf16[2048,3584]{1,0:T(8,128)(2,1)} fusion(bf16[2048,3584]{1,0:T(8,128)(2,1)} %param.6, f32[16,3584]{1,0:T(8,128)S(1)} %copy-done.5), kind=kLoop, calls=%fused_computation.1 | loop fusion | flops 22020096 | bytes 29589504 | tf_op jit(solution)/shard_map/convert_element_type | solution.py:344
  44.8 6.5 %all-gather.2.cloned.1.call-done = bf16[512,2048]{0,1:T(8,128)(2,1)} async-done(((bf16[512,512]{0,1:T(8,128)(2,1)}), bf16[512,2048]{0,1:T(8,128)(2,1)}) %all-gather.2.cloned.1.call-update) | async-done | bytes 2097168 | tf_op jit(solution)/shard_map/all_gather | solution.py:351
  51.3 4.0 %copy.14.tokens_ref = bf16[512,2048]{1,0:T(8,128)(2,1)} copy(bf16[512,2048]{0,1:T(8,128)(2,1)} %all-gather.2.cloned.1.call-done) | data formatting | bytes 4194304 | tf_op jit(solution)/shard_map/all_gather | solution.py:351
  55.3 115.2 %line_exchange.1 = (bf16[128,3584]{1,0:T(8,128)(2,1)}, bf16[512,3584]{1,0:T(8,128)(2,1)}, bf16[512,3584]{1,0:T(8,128)(2,1)}, bf16[512,2048]{1,0:T(8,128)(2,1)}, bf16[512,1024]{1,0:T(8,128)(2,1)}) custom-call(bf16[512,2048]{1,0:T(8,128)(2,1)} %copy.14.tokens_ref, bf16[2048,3584]{1,0:T(8,128)(2,1)} %fusion.weight_hbm, bf16[128,3584]{1,0:T(8,128)(2,1)} %cot_ref.1), custom_call_target="tpu_custom_call" | custom-call | tf_op jit(solution)/shard_map/line_exchange/pallas_call | solution.py:284
  170.5 0.0 copy-start.3
  170.5 1.4 dynamic-slice_bitcast_fusion
  171.9 0.1 collective-permute-start
  172.1 0.0 copy-start.6
  172.1 2.7 %collective-permute-done = bf16[2,128,2048]{2,1,0:T(8,128)(2,1)} collective-permute-done((bf16[2,128,2048]{2,1,0:T(8,128)(2,1)S(1)}, bf16[2,128,2048]{2,1,0:T(8,128)(2,1)}, u32[]{:S(2)}, u32[]{:S(2)}) %collective-permute-start) | collective-permute-done | bytes 1048608 | tf_op jit(solution)/shard_map/ppermute | solution.py:315
  174.8 0.0 copy-done.3
  174.8 1.6 fusion.1
  176.4 0.0 copy-start.1
  176.4 0.8 dynamic-slice_bitcast_fusion.1
  177.3 1.5 collective-permute-start.1
  178.7 0.0 copy-done.6
  178.8 0.1 fusion.6.table_ref
  178.9 2.3 copy.16
  181.2 0.0 copy-start.2
  181.2 0.0 copy-done.1
  181.2 0.1 constant_dynamic-slice_fusion
  181.2 1.1 copy-done.2
  182.4 0.0 copy-start
  182.4 0.3 maximum_bitcast_fusion.turned_ref
  182.7 8.8 %collective-permute-done.1 = bf16[128,2048]{1,0:T(8,128)(2,1)} collective-permute-done((bf16[128,2048]{1,0:T(8,128)(2,1)}, bf16[128,2048]{1,0:T(8,128)(2,1)}, u32[]{:S(2)}, u32[]{:S(2)}) %collective-permute-start.1) | collective-permute-done | bytes 524320 | tf_op jit(solution)/shard_map/ppermute | solution.py:315
  191.5 1.2 fusion.2
  192.7 5.2 %collective-permute-start.2 = (bf16[128,2048]{1,0:T(8,128)(2,1)S(1)}, bf16[128,2048]{1,0:T(8,128)(2,1)S(1)}, u32[]{:S(2)}, u32[]{:S(2)}) collective-permute-start(bf16[128,2048]{1,0:T(8,128)(2,1)S(1)} %fusion.2), channel_id=1, source_target_pairs={{0,0},{1,8},{2,16},{3,24},{8,1},{9,9},{10,17},{11,25},{16,2},{17,1... | collective-permute-start | bytes 1572872 | tf_op jit(solution)/shard_map/ppermute | solution.py:381
  198.0 0.0 copy-done
  198.0 0.0 copy-start.4
  198.0 13.3 %rotated_grad.1 = f32[1024,3584]{1,0:T(8,128)} custom-call(bf16[1024,1024]{1,0:T(8,128)(2,1)S(1)} %maximum_bitcast_fusion.turned_ref, bf16[512,3584]{1,0:T(8,128)(2,1)S(1)} %copy-done, bf16[512,3584]{1,0:T(8,128)(2,1)} %get-tuple-element.12.other_ref, bf16[1,3584]{1,0:T(2,128)(2,1)S(1)} %broadcast_in_dim.2.sign_ref, bf16[128,128]{1,0:T(8,128)(2,1)S(1)} %fusion.6.table_ref), custom_call_target="tpu_custom_call" | custom-call | flops 7516192768 | bytes 22020096 | tf_op jit(solution)/shard_map/rotated_grad/pallas_call | solution.py:42
  211.3 10.4 %collective-permute-done.2 = bf16[128,2048]{1,0:T(8,128)(2,1)S(1)} collective-permute-done((bf16[128,2048]{1,0:T(8,128)(2,1)S(1)}, bf16[128,2048]{1,0:T(8,128)(2,1)S(1)}, u32[]{:S(2)}, u32[]{:S(2)}) %collective-permute-start.2) | collective-permute-done | bytes 524320 | tf_op jit(solution)/shard_map/ppermute | solution.py:381
  221.7 0.0 copy-done.4
  221.7 0.9 copy.22
  222.6 0.8 copy.23
  (3 shorter events, 0.1 us)
Async XLA Ops:
  7.2 44.2 %all-gather.2.cloned.1.call-start = ((), (), s32[]{:S(2)}) async-start(), calls=%async_computation.1 | async-start | bytes 2621440 | tf_op jit(solution)/shard_map/all_gather | solution.py:351
  10.4 20.3 %copy-start.5 = (f32[16,3584]{1,0:T(8,128)S(1)}, f32[16,3584]{1,0:T(8,128)}, u32[]{:S(2)}) copy-start(f32[16,3584]{1,0:T(8,128)} %param.7) | copy-start | bytes 688132
  170.5 4.3 %copy-start.3 = (bf16[512,2048]{1,0:T(8,128)(2,1)S(1)}, bf16[512,2048]{1,0:T(8,128)(2,1)}, u32[]{:S(2)}) copy-start(bf16[512,2048]{1,0:T(8,128)(2,1)} %get-tuple-element.9) | copy-start | bytes 6291460
  171.9 2.9 %collective-permute-start = (bf16[2,128,2048]{2,1,0:T(8,128)(2,1)S(1)}, bf16[2,128,2048]{2,1,0:T(8,128)(2,1)}, u32[]{:S(2)}, u32[]{:S(2)}) collective-permute-start(bf16[2,128,2048]{2,1,0:T(8,128)(2,1)S(1)} %dynamic-slice_bitcast_fusion), channel_id=1, source_target_pairs={{0,1},{1,0},{2,3},{3,2},{4,5},{5,4},{6,7},{7,6},{8,9},{9,8},{10,11... | collective-permute-start | bytes 3145736 | tf_op jit(solution)/shard_map/ppermute | solution.py:315
  172.1 6.7 %copy-start.6 = (s32[3584]{0:T(1024)S(1)}, s32[3584]{0:T(1024)}, u32[]{:S(2)}) copy-start(s32[3584]{0:T(1024)} %param.9) | copy-start | bytes 43012
  176.4 4.7 %copy-start.1 = (bf16[512,2048]{0,1:T(8,128)(2,1)S(1)}, bf16[512,2048]{0,1:T(8,128)(2,1)}, u32[]{:S(2)}) copy-start(bf16[512,2048]{0,1:T(8,128)(2,1)} %all-gather.2.cloned.1.call-done) | copy-start | bytes 6291460
  177.3 14.3 %collective-permute-start.1 = (bf16[128,2048]{1,0:T(8,128)(2,1)}, bf16[128,2048]{1,0:T(8,128)(2,1)}, u32[]{:S(2)}, u32[]{:S(2)}) collective-permute-start(bf16[128,2048]{1,0:T(8,128)(2,1)} %dynamic-slice_bitcast_fusion.1), channel_id=1, source_target_pairs={{0,2},{1,3},{2,0},{3,1},{4,6},{5,7},{6,4},{7,5},{8,10},{9,11},{10,... | collective-permute-start | bytes 1572872 | tf_op jit(solution)/shard_map/ppermute | solution.py:315
  181.2 1.2 copy-start.2
  182.4 15.6 %copy-start = (bf16[512,3584]{1,0:T(8,128)(2,1)S(1)}, bf16[512,3584]{1,0:T(8,128)(2,1)}, u32[]{:S(2)}) copy-start(bf16[512,3584]{1,0:T(8,128)(2,1)} %get-tuple-element.11.mine_ref) | copy-start | bytes 11010052
  192.7 29.0 %collective-permute-start.2 = (bf16[128,2048]{1,0:T(8,128)(2,1)S(1)}, bf16[128,2048]{1,0:T(8,128)(2,1)S(1)}, u32[]{:S(2)}, u32[]{:S(2)}) collective-permute-start(bf16[128,2048]{1,0:T(8,128)(2,1)S(1)} %fusion.2), channel_id=1, source_target_pairs={{0,0},{1,8},{2,16},{3,24},{8,1},{9,9},{10,17},{11,25},{16,2},{17,1... | collective-permute-start | bytes 1572872 | tf_op jit(solution)/shard_map/ppermute | solution.py:381
  198.0 23.7 %copy-start.4 = (bf16[128,3584]{1,0:T(8,128)(2,1)S(1)}, bf16[128,3584]{1,0:T(8,128)(2,1)}, u32[]{:S(2)}) copy-start(bf16[128,3584]{1,0:T(8,128)(2,1)} %get-tuple-element.16) | copy-start | bytes 2752516
Sparse Core Ops, SparseCore 0:
  30.8 20.4 all-gather.1

commit v4 on v3

--- a/solution.py
+++ b/solution.py
@@ -63,6 +63,140 @@
 MESH = pl.DeviceIdType.MESH
 
 
+def fetch_kernel(
+    n, tokens_ref, codes_ref, scales_ref, weight_ref, columns_ref, came,
+    out_sent, out_came, mate_sent, mate_came, over_sent, over_came, relay_sent, relay_came,
+):
+    step, last = pl.program_id(0), pl.num_programs(0) - 1
+    me, t = lax.axis_index("fsdp"), lax.axis_index("tensor")
+    mate, over = t + 1 - 2 * (t % 2), (t + 2) % 4
+    rows = tokens_ref.shape[0]
+    depth = tokens_ref.shape[1] // n
+    piece = depth // 4
+
+    def spot(s, q):
+        return came.at[
+            pl.ds(pl.multiple_of(s * rows, rows), rows), pl.ds(pl.multiple_of(q * piece, piece), piece)
+        ]
+
+    def send_out(f):
+        start = pl.multiple_of(f * depth + t * piece, piece)
+        return pltpu.make_async_remote_copy(
+            src_ref=tokens_ref.at[:, pl.ds(start, piece)], dst_ref=spot(me, t),
+            send_sem=out_sent.at[f], recv_sem=out_came.at[me],
+            device_id={"fsdp": f}, device_id_type=MESH,
+        )
+
+    def receive_out(s):
+        return pltpu.make_async_remote_copy(
+            src_ref=spot(s, t), dst_ref=spot(s, t),
+            send_sem=out_sent.at[s], recv_sem=out_came.at[s],
+            device_id={"fsdp": s}, device_id_type=MESH,
+        )
+
+    def pass_on(s, q, sent, arrival, device):
+        return pltpu.make_async_remote_copy(
+            src_ref=spot(s, q), dst_ref=spot(s, q), send_sem=sent.at[s], recv_sem=arrival.at[s],
+            device_id={"tensor": device}, device_id_type=MESH,
+        )
+
+    def to_mate(s):
+        return pass_on(s, t, mate_sent, mate_came, mate)
+
+    def to_over(s):
+        return pass_on(s, t, over_sent, over_came, over)
+
+    def to_relay(s):
+        return pass_on(s, over, relay_sent, relay_came, mate)
+
+    @pl.when(step == 0)
+    def _():
+        barrier = pltpu.get_barrier_semaphore()
+        for k in range(1, n):
+            pl.semaphore_signal(barrier, inc=1, device_id={"fsdp": (me + k) % n}, device_id_type=MESH)
+        pl.semaphore_signal(barrier, inc=1, device_id={"tensor": mate}, device_id_type=MESH)
+        pl.semaphore_signal(barrier, inc=1, device_id={"tensor": over}, device_id_type=MESH)
+        pl.semaphore_wait(barrier, n + 1)
+        for k in range(1, n):
+            send_out((me + k) % n).start()
+        came[pl.ds(pl.multiple_of(me * rows, rows), rows), :] = tokens_ref[
+            :, pl.ds(pl.multiple_of(me * depth, depth), depth)
+        ]
+
+    weight_ref[...] = (
+        codes_ref[...].astype(jnp.float32) * scales_ref[pl.ds(step, 1), :]
+    ).astype(jnp.bfloat16)
+
+    def each(k, act):
+        for s in (me - k, me + k):
+            @pl.when(jnp.logical_and(s >= 0, s < n))
+            def _():
+                act(s)
+
+    def forward(s):
+        receive_out(s).wait_recv()
+        to_mate(s).start()
+        to_over(s).start()
+
+    def relay(s):
+        to_over(s).wait_recv()
+        to_relay(s).start()
+
+    for k in range(1, n):
+        @pl.when(step == jnp.minimum(2 + 3 * k, last))
+        def _():
+            each(k, forward)
+
+    for k in range(1, n):
+        @pl.when(step == jnp.minimum(5 + 3 * k, last))
+        def _():
+            each(k, relay)
+
+    def finish(s):
+        to_mate(s).wait_recv()
+        to_relay(s).wait_recv()
+        send_out(s).wait_send()
+        to_mate(s).wait_send()
+        to_over(s).wait_send()
+        to_relay(s).wait_send()
+
+    @pl.when(step == last)
+    def _():
+        for k in range(1, n):
+            each(k, finish)
+        columns_ref[...] = came[...]
+
+
+def fetch_tokens(tokens, codes, scales, n):
+    rows, width = tokens.shape
+    shard_rows, cols = codes.shape
+    steps = scales.shape[0]
+    fixed = lambda i: (0, 0)
+    sem = pltpu.SemaphoreType.DMA((n,))
+    return pl.pallas_call(
+        functools.partial(fetch_kernel, n),
+        grid=(steps,),
+        out_shape=(
+            jax.ShapeDtypeStruct(codes.shape, jnp.bfloat16),
+            jax.ShapeDtypeStruct((n * rows, shard_rows), jnp.bfloat16),
+        ),
+        in_specs=[
+            pl.BlockSpec((rows, width), fixed),
+            pl.BlockSpec((shard_rows // steps, cols), lambda i: (i, 0)),
+            pl.BlockSpec((steps, cols), fixed),
+        ],
+        out_specs=(
+            pl.BlockSpec((shard_rows // steps, cols), lambda i: (i, 0)),
+            pl.BlockSpec((n * rows, shard_rows), fixed),
+        ),
+        scratch_shapes=[pltpu.VMEM((n * rows, shard_rows), jnp.bfloat16)] + [sem] * 8,
+        compiler_params=pltpu.CompilerParams(
+            collective_id=1, has_side_effects=True, vmem_limit_bytes=48 * 1024 * 1024
+        ),
+        name="fetch_tokens",
+    )(tokens, codes, scales)
+
+
 def line_kernel(
     n, width, tokens_ref, weight_hbm, cot_ref, act_ref, mine_ref, other_ref, product_ref, across_ref,
     part_ref, sums, from_left, from_right, total, weight_ref, gathered, fetched, swap_sent, swap_came,
@@ -335,20 +469,23 @@
     local_tokens = tokens.shape[0]
     shard_rows, hidden_cols = weight_codes.shape
     block_rows = shard_rows // scales.shape[0]
-    weight = (
-        (
-            weight_codes.astype(jnp.float32).reshape(scales.shape[0], block_rows, hidden_cols)
-            * scales[:, None, :]
-        )
-        .reshape(shard_rows, hidden_cols)
-        .astype(jnp.bfloat16)
-    )
-    piece = shard_rows // n_tensor
-    own = lax.dynamic_slice_in_dim(
-        tokens.reshape(local_tokens, n_fsdp, shard_rows), lax.axis_index("tensor") * piece, piece, 2
-    ).reshape(local_tokens, n_fsdp * piece)
-    quarter = lax.all_to_all(own, "fsdp", split_axis=1, concat_axis=0, tiled=True)
-    columns = lax.all_gather(quarter, "tensor", axis=1, tiled=True)
+    if n_tensor == 4 and 1 < n_fsdp <= 4:
+        weight, columns = fetch_tokens(tokens, weight_codes, scales, n_fsdp)
+    else:
+        weight = (
+            (
+                weight_codes.astype(jnp.float32).reshape(scales.shape[0], block_rows, hidden_cols)
+                * scales[:, None, :]
+            )
+            .reshape(shard_rows, hidden_cols)
+            .astype(jnp.bfloat16)
+        )
+        piece = shard_rows // n_tensor
+        own = lax.dynamic_slice_in_dim(
+            tokens.reshape(local_tokens, n_fsdp, shard_rows), lax.axis_index("tensor") * piece, piece, 2
+        ).reshape(local_tokens, n_fsdp * piece)
+        quarter = lax.all_to_all(own, "fsdp", split_axis=1, concat_axis=0, tiled=True)
+        columns = lax.all_gather(quarter, "tensor", axis=1, tiled=True)
     half_rows = shard_rows // 2
     replica = lax.axis_index("replica")
     kept = lax.dynamic_slice_in_dim(columns, replica * half_rows, half_rows, 1)

time: 231 us -> 200 us (0.87)
  Pallas kernels: 128 us -> 156 us
  blocking collectives: 19.3 us -> 0 us
  other arithmetic: 17.3 us -> 3.5 us
  between operations: 14.2 us -> 0.85 us
  waiting for transfers between devices: 28.5 us -> 20.2 us
    pallas_call x0 -> x1, Pallas kernels: none -> 26.3 us  [fetch_tokens(): pl.pallas_call(functools.partial(fetch_kernel, n), grid=(steps,), out_sha...]
    all_to_all x1 -> x0, blocking collectives: 19.3 us -> none  [shards(): lax.all_to_all(own, 'fsdp', split_axis=1, concat_axis=0, tiled=True)]
    convert_element_type x1 -> x0, other arithmetic: 14.1 us -> none  [shards(): weight = (weight_codes.astype(jnp.float32).reshape(scales.shape[0], block...]
    all_gather x1 -> x0, waiting for transfers between devices: 6.49 us -> none  [shards(): columns = lax.all_gather(quarter, 'tensor', axis=1, tiled=True)]
    all_gather x1 -> x0, local copies, waits for them, and re-layouts: 3.97 us -> none  [shards(): columns = lax.all_gather(quarter, 'tensor', axis=1, tiled=True)]
    pallas_call x0 -> x1, local copies, waits for them, and re-layouts: none -> 2.5 us  [fetch_tokens(): pl.pallas_call(functools.partial(fetch_kernel, n), grid=(steps,), out_sha...]
    unnamed x17 -> x20, local copies, waits for them, and re-layouts: 6.12 us -> 6.6 us
  transfers between devices with their start and end apart: 4 -> 3, of which waited for: 4 -> 3; matrix products, arithmetic and copies ran while one was open for 7% -> 3% of each run, Pallas kernels for 6% -> 7%
where the time goes in v4:
time: 200 us; the launch traced here: 199 us
  Pallas kernels  156 us (78%)
  waiting for transfers between devices  20.2 us (10%)
  local copies, waits for them, and re-layouts  13.8 us (7%)
  starting transfers between devices  5.03 us (3%)
  other arithmetic  3.5 us (2%)
    pallas_call x1, Pallas kernels, line_exchange(): pl.pallas_call(functools.partial(line_kernel, n, width), out_shape=(jax.S...  116 us
    pallas_call x1, Pallas kernels, fetch_tokens(): pl.pallas_call(functools.partial(fetch_kernel, n), grid=(steps,), out_sha...  26.3 us
    pallas_call x1, Pallas kernels, rotated_grad(): pl.pallas_call(functools.partial(grad_kernel, scaling), grid=(width // ti...  13.3 us
    ppermute x1, waiting for transfers between devices, shards(): input_grad = lax.ppermute(summed, ('fsdp', 'tensor'), swap)  10.8 us
    ppermute x2, waiting for transfers between devices, halve(): came = lax.ppermute(sent, 'tensor', [(t, t ^ bit) for t in range(n_tensor)])  9.42 us
    unnamed x20, local copies, waits for them, and re-layouts  6.6 us
  transfers between devices with their start and end apart: 3, of which 3 were waited for; matrix products, arithmetic and copies ran while one was open for 3% of the time, Pallas kernels for 7%

profile of v4, /device:TPU:4, one launch (start us, length us, event | category | flops | bytes accessed | tf_op | source)
XLA Modules:
  0.0 199.0 jit_solution(7991380258026980001)
XLA Ops:
  0.7 0.0 copy-start.2
  0.7 1.6 copy-done.2
  2.2 0.0 copy-start.3
  2.2 0.9 copy-done.3
  3.2 26.3 %fetch_tokens.1 = (bf16[2048,3584]{1,0:T(8,128)(2,1)}, bf16[512,2048]{1,0:T(8,128)(2,1)S(1)}) custom-call(bf16[128,8192]{1,0:T(8,128)(2,1)S(1)} %copy-done.2, bf16[2048,3584]{1,0:T(8,128)(2,1)} %codes_ref.1, f32[16,3584]{1,0:T(8,128)S(1)} %copy-done.3), custom_call_target="tpu_custom_call" | custom-call | tf_op jit(solution)/shard_map/fetch_tokens/pallas_call | solution.py:176
  29.5 0.0 copy-start
  29.5 1.3 copy-done
  30.8 116.1 %line_exchange.1 = (bf16[128,3584]{1,0:T(8,128)(2,1)}, bf16[512,3584]{1,0:T(8,128)(2,1)}, bf16[512,3584]{1,0:T(8,128)(2,1)}, bf16[512,2048]{1,0:T(8,128)(2,1)}, bf16[512,1024]{1,0:T(8,128)(2,1)}) custom-call(bf16[512,2048]{1,0:T(8,128)(2,1)} %copy-done, bf16[2048,3584]{1,0:T(8,128)(2,1)} %get-tuple-element.11.weight_hbm, bf16[128,3584]{1,0:T(8,128)(2,1)} %cot_ref.1), custom_call_target="tpu_custom_call" | custom-call | tf_op jit(solution)/shard_map/line_exchange/pallas_call | solution.py:418
  146.9 1.3 dynamic-slice_bitcast_fusion
  148.2 0.1 collective-permute-start
  148.3 0.0 copy-start.8
  148.3 0.0 copy-start.1
  148.3 2.7 %collective-permute-done = bf16[2,128,2048]{2,1,0:T(8,128)(2,1)} collective-permute-done((bf16[2,128,2048]{2,1,0:T(8,128)(2,1)S(1)}, bf16[2,128,2048]{2,1,0:T(8,128)(2,1)}, u32[]{:S(2)}, u32[]{:S(2)}) %collective-permute-start) | collective-permute-done | bytes 1048608 | tf_op jit(solution)/shard_map/ppermute | solution.py:449
  151.1 1.9 fusion
  153.0 0.8 dynamic-slice_bitcast_fusion.1
  153.8 1.1 collective-permute-start.1
  154.9 0.0 copy-done.8
  154.9 0.0 copy-done.1
  154.9 2.5 %copy.9 = bf16[512,2048]{0,1:T(8,128)(2,1)} copy(bf16[512,2048]{1,0:T(8,128)(2,1)S(1)} %copy-done.1) | data formatting | bytes 4194304 | tf_op jit(solution)/shard_map/fetch_tokens/pallas_call | solution.py:176
  157.4 0.0 copy-start.5
  157.4 2.4 %copy.10 = bf16[512,1024]{0,1:T(8,128)(2,1)} copy(bf16[512,1024]{1,0:T(8,128)(2,1)} %get-tuple-element.14) | data formatting | bytes 2097152 | tf_op jit(solution)/shard_map/line_exchange/pallas_call | solution.py:418
  159.9 0.0 copy-start.6
  159.9 0.1 fusion.5.table_ref
  160.0 0.0 copy-done.5
  160.0 0.1 constant_dynamic-slice_fusion
  160.1 1.0 copy-done.6
  161.1 0.0 copy-start.4
  161.1 0.3 maximum_bitcast_fusion.turned_ref
  161.4 6.7 %collective-permute-done.1 = bf16[128,2048]{1,0:T(8,128)(2,1)} collective-permute-done((bf16[128,2048]{1,0:T(8,128)(2,1)}, bf16[128,2048]{1,0:T(8,128)(2,1)}, u32[]{:S(2)}, u32[]{:S(2)}) %collective-permute-start.1) | collective-permute-done | bytes 524320 | tf_op jit(solution)/shard_map/ppermute | solution.py:449
  168.1 1.2 fusion.1
  169.3 3.9 %collective-permute-start.2 = (bf16[128,2048]{1,0:T(8,128)(2,1)S(1)}, bf16[128,2048]{1,0:T(8,128)(2,1)S(1)}, u32[]{:S(2)}, u32[]{:S(2)}) collective-permute-start(bf16[128,2048]{1,0:T(8,128)(2,1)S(1)} %fusion.1), channel_id=1, source_target_pairs={{0,0},{1,8},{2,16},{3,24},{8,1},{9,9},{10,17},{11,25},{16,2},{17,1... | collective-permute-start | bytes 1572872 | tf_op jit(solution)/shard_map/ppermute | solution.py:518
  173.2 0.0 copy-done.4
  173.2 0.0 copy-start.7
  173.2 13.3 %rotated_grad.1 = f32[1024,3584]{1,0:T(8,128)} custom-call(bf16[1024,1024]{1,0:T(8,128)(2,1)S(1)} %maximum_bitcast_fusion.turned_ref, bf16[512,3584]{1,0:T(8,128)(2,1)S(1)} %copy-done.4, bf16[512,3584]{1,0:T(8,128)(2,1)} %get-tuple-element.16.other_ref, bf16[1,3584]{1,0:T(2,128)(2,1)S(1)} %broadcast_in_dim.2.sign_ref, bf16[128,128]{1,0:T(8,128)(2,1)S(1)} %fusion.5.table_ref), custom_call_target="tpu_custom_call" | custom-call | flops 7516192768 | bytes 22020096 | tf_op jit(solution)/shard_map/rotated_grad/pallas_call | solution.py:42
  186.5 10.8 %collective-permute-done.2 = bf16[128,2048]{1,0:T(8,128)(2,1)S(1)} collective-permute-done((bf16[128,2048]{1,0:T(8,128)(2,1)S(1)}, bf16[128,2048]{1,0:T(8,128)(2,1)S(1)}, u32[]{:S(2)}, u32[]{:S(2)}) %collective-permute-start.2) | collective-permute-done | bytes 524320 | tf_op jit(solution)/shard_map/ppermute | solution.py:518
  197.3 0.0 copy-done.7
  197.3 0.9 copy.14
  198.2 0.8 copy.15
  (2 shorter events, 0.0 us)
Async XLA Ops:
  0.7 1.6 copy-start.2
  2.2 0.9 copy-start.3
  29.5 1.3 copy-start
  148.2 2.9 %collective-permute-start = (bf16[2,128,2048]{2,1,0:T(8,128)(2,1)S(1)}, bf16[2,128,2048]{2,1,0:T(8,128)(2,1)}, u32[]{:S(2)}, u32[]{:S(2)}) collective-permute-start(bf16[2,128,2048]{2,1,0:T(8,128)(2,1)S(1)} %dynamic-slice_bitcast_fusion), channel_id=1, source_target_pairs={{0,1},{1,0},{2,3},{3,2},{4,5},{5,4},{6,7},{7,6},{8,9},{9,8},{10,11... | collective-permute-start | bytes 3145736 | tf_op jit(solution)/shard_map/ppermute | solution.py:449
  148.3 6.6 %copy-start.8 = (s32[3584]{0:T(1024)S(1)}, s32[3584]{0:T(1024)}, u32[]{:S(2)}) copy-start(s32[3584]{0:T(1024)} %param.9) | copy-start | bytes 43012
  148.3 6.6 %copy-start.1 = (bf16[512,2048]{1,0:T(8,128)(2,1)S(1)}, bf16[512,2048]{1,0:T(8,128)(2,1)}, u32[]{:S(2)}) copy-start(bf16[512,2048]{1,0:T(8,128)(2,1)} %copy-done) | copy-start | bytes 6291460
  153.8 14.3 %collective-permute-start.1 = (bf16[128,2048]{1,0:T(8,128)(2,1)}, bf16[128,2048]{1,0:T(8,128)(2,1)}, u32[]{:S(2)}, u32[]{:S(2)}) collective-permute-start(bf16[128,2048]{1,0:T(8,128)(2,1)} %dynamic-slice_bitcast_fusion.1), channel_id=1, source_target_pairs={{0,2},{1,3},{2,0},{3,1},{4,6},{5,7},{6,4},{7,5},{8,10},{9,11},{10,... | collective-permute-start | bytes 1572872 | tf_op jit(solution)/shard_map/ppermute | solution.py:449
  157.4 2.6 %copy-start.5 = (bf16[512,2048]{0,1:T(8,128)(2,1)S(1)}, bf16[512,2048]{0,1:T(8,128)(2,1)}, u32[]{:S(2)}) copy-start(bf16[512,2048]{0,1:T(8,128)(2,1)} %copy.9) | copy-start | bytes 6291460
  159.9 1.2 copy-start.6
  161.1 12.1 %copy-start.4 = (bf16[512,3584]{1,0:T(8,128)(2,1)S(1)}, bf16[512,3584]{1,0:T(8,128)(2,1)}, u32[]{:S(2)}) copy-start(bf16[512,3584]{1,0:T(8,128)(2,1)} %get-tuple-element.15.mine_ref) | copy-start | bytes 11010052
  169.3 28.0 %collective-permute-start.2 = (bf16[128,2048]{1,0:T(8,128)(2,1)S(1)}, bf16[128,2048]{1,0:T(8,128)(2,1)S(1)}, u32[]{:S(2)}, u32[]{:S(2)}) collective-permute-start(bf16[128,2048]{1,0:T(8,128)(2,1)S(1)} %fusion.1), channel_id=1, source_target_pairs={{0,0},{1,8},{2,16},{3,24},{8,1},{9,9},{10,17},{11,25},{16,2},{17,1... | collective-permute-start | bytes 1572872 | tf_op jit(solution)/shard_map/ppermute | solution.py:518
  173.2 24.1 %copy-start.7 = (bf16[128,3584]{1,0:T(8,128)(2,1)S(1)}, bf16[128,3584]{1,0:T(8,128)(2,1)}, u32[]{:S(2)}) copy-start(bf16[128,3584]{1,0:T(8,128)(2,1)} %get-tuple-element.20) | copy-start | bytes 2752516

commit v5 on v4

--- a/solution.py
+++ b/solution.py
@@ -199,11 +199,12 @@
 
 def line_kernel(
     n, width, tokens_ref, weight_hbm, cot_ref, act_ref, mine_ref, other_ref, product_ref, across_ref,
-    part_ref, sums, from_left, from_right, total, weight_ref, gathered, fetched, swap_sent, swap_came,
+    part_ref, sums, from_left, from_right, total, weight_ref, gathered, fetched, swap_sent, swap_came, pair_sent, pair_came,
     sum_sent, left_came, right_came, up_sent, down_sent, came, cross_sent, cross_came,
 ):
     me = lax.axis_index("fsdp")
     partner_id = 1 - lax.axis_index("replica")
+    mate = lax.axis_index("tensor") + 1 - 2 * (lax.axis_index("tensor") % 2)
     high = jnp.minimum(me + 1, n - 1)
     low = jnp.maximum(me - 1, 0)
     rows = cot_ref.shape[0]
@@ -258,6 +259,7 @@
 
     barrier = pltpu.get_barrier_semaphore()
     pl.semaphore_signal(barrier, inc=1, device_id={"replica": partner_id}, device_id_type=MESH)
+    pl.semaphore_signal(barrier, inc=1, device_id={"tensor": mate}, device_id_type=MESH)
 
     @pl.when(has_low)
     def _():
@@ -267,13 +269,21 @@
     def _():
         pl.semaphore_signal(barrier, inc=1, device_id={"fsdp": high}, device_id_type=MESH)
 
-    pl.semaphore_wait(barrier, 1 + jnp.where(has_low, 1, 0) + jnp.where(has_high, 1, 0))
+    pl.semaphore_wait(barrier, 2 + jnp.where(has_low, 1, 0) + jnp.where(has_high, 1, 0))
 
     depth = across_ref.shape[1]
+    small = depth // 2
+    lane = lax.axis_index("tensor") % 2
+    share = across_ref.at[:, pl.ds(pl.multiple_of(lane * small, small), small)]
+    start = pl.multiple_of(partner_id * depth + lane * small, small)
     swap = pltpu.make_async_remote_copy(
-        src_ref=tokens_ref.at[:, pl.ds(pl.multiple_of(partner_id * depth, depth), depth)],
-        dst_ref=across_ref, send_sem=swap_sent, recv_sem=swap_came,
+        src_ref=tokens_ref.at[:, pl.ds(start, small)],
+        dst_ref=share, send_sem=swap_sent, recv_sem=swap_came,
         device_id={"replica": partner_id}, device_id_type=MESH,
+    )
+    pair = pltpu.make_async_remote_copy(
+        src_ref=share, dst_ref=share, send_sem=pair_sent, recv_sem=pair_came,
+        device_id={"tensor": mate}, device_id_type=MESH,
     )
     swap.start()
     gathered[...] = jnp.zeros_like(gathered)
@@ -366,6 +376,11 @@
 
                 cross(s, late).start()
 
+        @pl.when(i == blocks - 1)
+        def _():
+            swap.wait()
+            pair.start()
+
         @pl.when(i + 1 < blocks)
         def _():
             project(i + 1)
@@ -385,7 +400,7 @@
     lax.fori_loop(0, blocks + 2 * (n - 1), step, 0)
 
     product_ref[...] = gathered[...].astype(jnp.bfloat16)
-    swap.wait()
+    pair.wait()
 
     def drain(c, carry):
         for d in range(n):
@@ -434,6 +449,8 @@
             pltpu.SemaphoreType.DMA((cols // width,)),
             pltpu.SemaphoreType.DMA,
             pltpu.SemaphoreType.DMA,
+            pltpu.SemaphoreType.DMA,
+            pltpu.SemaphoreType.DMA,
         ]
         + [sems] * 8,
         compiler_params=pltpu.CompilerParams(
@@ -491,7 +508,7 @@
     kept = lax.dynamic_slice_in_dim(columns, replica * half_rows, half_rows, 1)
     gathered = n_fsdp * local_tokens
     held = 2 * shard_rows * hidden_cols + 12 * gathered * hidden_cols + 9 * gathered * shard_rows
-    if n_fsdp > 1 and held <= 52 * 1024 * 1024:
+    if n_fsdp > 1 and n_tensor % 2 == 0 and held <= 52 * 1024 * 1024:
         activation, arrived, other, product, across = line_exchange(columns, weight, cotangent, n_fsdp)
     else:
         across = partner(lax.dynamic_slice_in_dim(columns, (1 - replica) * half_rows, half_rows, 1))

time: 200 us -> 197 us (0.985)
  Pallas kernels: 156 us -> 152 us
    pallas_call x1, Pallas kernels: 116 us -> 113 us  [line_exchange(): pl.pallas_call(functools.partial(line_kernel, n, width), out_shape=(jax.S...]
where the time goes in v5:
time: 197 us; the launch traced here: 196 us
  Pallas kernels  152 us (77%)
  waiting for transfers between devices  21.9 us (11%)
  local copies, waits for them, and re-layouts  13.8 us (7%)
  starting transfers between devices  4.09 us (2%)
  other arithmetic  3.5 us (2%)
    pallas_call x1, Pallas kernels, line_exchange(): pl.pallas_call(functools.partial(line_kernel, n, width), out_shape=(jax.S...  113 us
    pallas_call x1, Pallas kernels, fetch_tokens(): pl.pallas_call(functools.partial(fetch_kernel, n), grid=(steps,), out_sha...  26.3 us
    pallas_call x1, Pallas kernels, rotated_grad(): pl.pallas_call(functools.partial(grad_kernel, scaling), grid=(width // ti...  13.3 us
    ppermute x1, waiting for transfers between devices, shards(): input_grad = lax.ppermute(summed, ('fsdp', 'tensor'), swap)  12.4 us
    ppermute x2, waiting for transfers between devices, halve(): came = lax.ppermute(sent, 'tensor', [(t, t ^ bit) for t in range(n_tensor)])  9.45 us
    unnamed x20, local copies, waits for them, and re-layouts  6.6 us
  transfers between devices with their start and end apart: 3, of which 3 were waited for; matrix products, arithmetic and copies ran while one was open for 3% of the time, Pallas kernels for 7%

profile of v5, /device:TPU:4, one launch (start us, length us, event | category | flops | bytes accessed | tf_op | source)
XLA Modules:
  0.0 196.4 jit_solution(8767853878524928899)
XLA Ops:
  0.7 0.0 copy-start.2
  0.7 1.6 copy-done.2
  2.2 0.0 copy-start.3
  2.2 0.9 copy-done.3
  3.2 26.3 %fetch_tokens.1 = (bf16[2048,3584]{1,0:T(8,128)(2,1)}, bf16[512,2048]{1,0:T(8,128)(2,1)S(1)}) custom-call(bf16[128,8192]{1,0:T(8,128)(2,1)S(1)} %copy-done.2, bf16[2048,3584]{1,0:T(8,128)(2,1)} %codes_ref.1, f32[16,3584]{1,0:T(8,128)S(1)} %copy-done.3), custom_call_target="tpu_custom_call" | custom-call | tf_op jit(solution)/shard_map/fetch_tokens/pallas_call | solution.py:176
  29.5 0.0 copy-start
  29.5 1.3 copy-done
  30.8 112.7 %line_exchange.1 = (bf16[128,3584]{1,0:T(8,128)(2,1)}, bf16[512,3584]{1,0:T(8,128)(2,1)}, bf16[512,3584]{1,0:T(8,128)(2,1)}, bf16[512,2048]{1,0:T(8,128)(2,1)}, bf16[512,1024]{1,0:T(8,128)(2,1)}) custom-call(bf16[512,2048]{1,0:T(8,128)(2,1)} %copy-done, bf16[2048,3584]{1,0:T(8,128)(2,1)} %get-tuple-element.11.weight_hbm, bf16[128,3584]{1,0:T(8,128)(2,1)} %cot_ref.1), custom_call_target="tpu_custom_call" | custom-call | tf_op jit(solution)/shard_map/line_exchange/pallas_call | solution.py:433
  143.5 1.3 dynamic-slice_bitcast_fusion
  144.8 0.1 collective-permute-start
  144.9 0.0 copy-start.8
  145.0 0.0 copy-start.1
  145.0 2.7 %collective-permute-done = bf16[2,128,2048]{2,1,0:T(8,128)(2,1)} collective-permute-done((bf16[2,128,2048]{2,1,0:T(8,128)(2,1)S(1)}, bf16[2,128,2048]{2,1,0:T(8,128)(2,1)}, u32[]{:S(2)}, u32[]{:S(2)}) %collective-permute-start) | collective-permute-done | bytes 1048608 | tf_op jit(solution)/shard_map/ppermute | solution.py:466
  147.7 1.9 fusion
  149.6 0.8 dynamic-slice_bitcast_fusion.1
  150.5 1.0 collective-permute-start.1
  151.5 0.0 copy-done.8
  151.5 0.0 copy-done.1
  151.5 2.5 %copy.9 = bf16[512,2048]{0,1:T(8,128)(2,1)} copy(bf16[512,2048]{1,0:T(8,128)(2,1)S(1)} %copy-done.1) | data formatting | bytes 4194304 | tf_op jit(solution)/shard_map/fetch_tokens/pallas_call | solution.py:176
  154.0 0.0 copy-start.5
  154.0 2.4 %copy.10 = bf16[512,1024]{0,1:T(8,128)(2,1)} copy(bf16[512,1024]{1,0:T(8,128)(2,1)} %get-tuple-element.14) | data formatting | bytes 2097152 | tf_op jit(solution)/shard_map/line_exchange/pallas_call | solution.py:433
  156.5 0.0 copy-start.6
  156.5 0.1 fusion.5.table_ref
  156.6 0.0 copy-done.5
  156.6 0.1 constant_dynamic-slice_fusion
  156.7 1.0 copy-done.6
  157.7 0.0 copy-start.4
  157.7 0.3 maximum_bitcast_fusion.turned_ref
  158.0 6.7 %collective-permute-done.1 = bf16[128,2048]{1,0:T(8,128)(2,1)} collective-permute-done((bf16[128,2048]{1,0:T(8,128)(2,1)}, bf16[128,2048]{1,0:T(8,128)(2,1)}, u32[]{:S(2)}, u32[]{:S(2)}) %collective-permute-start.1) | collective-permute-done | bytes 524320 | tf_op jit(solution)/shard_map/ppermute | solution.py:466
  164.7 1.2 fusion.1
  165.9 3.0 %collective-permute-start.2 = (bf16[128,2048]{1,0:T(8,128)(2,1)S(1)}, bf16[128,2048]{1,0:T(8,128)(2,1)S(1)}, u32[]{:S(2)}, u32[]{:S(2)}) collective-permute-start(bf16[128,2048]{1,0:T(8,128)(2,1)S(1)} %fusion.1), channel_id=1, source_target_pairs={{0,0},{1,8},{2,16},{3,24},{8,1},{9,9},{10,17},{11,25},{16,2},{17,1... | collective-permute-start | bytes 1572872 | tf_op jit(solution)/shard_map/ppermute | solution.py:535
  168.9 0.0 copy-done.4
  168.9 0.0 copy-start.7
  168.9 13.3 %rotated_grad.1 = f32[1024,3584]{1,0:T(8,128)} custom-call(bf16[1024,1024]{1,0:T(8,128)(2,1)S(1)} %maximum_bitcast_fusion.turned_ref, bf16[512,3584]{1,0:T(8,128)(2,1)S(1)} %copy-done.4, bf16[512,3584]{1,0:T(8,128)(2,1)} %get-tuple-element.16.other_ref, bf16[1,3584]{1,0:T(2,128)(2,1)S(1)} %broadcast_in_dim.2.sign_ref, bf16[128,128]{1,0:T(8,128)(2,1)S(1)} %fusion.5.table_ref), custom_call_target="tpu_custom_call" | custom-call | flops 7516192768 | bytes 22020096 | tf_op jit(solution)/shard_map/rotated_grad/pallas_call | solution.py:42
  182.2 12.4 %collective-permute-done.2 = bf16[128,2048]{1,0:T(8,128)(2,1)S(1)} collective-permute-done((bf16[128,2048]{1,0:T(8,128)(2,1)S(1)}, bf16[128,2048]{1,0:T(8,128)(2,1)S(1)}, u32[]{:S(2)}, u32[]{:S(2)}) %collective-permute-start.2) | collective-permute-done | bytes 524320 | tf_op jit(solution)/shard_map/ppermute | solution.py:535
  194.7 0.0 copy-done.7
  194.7 0.9 copy.14
  195.6 0.8 copy.15
  (2 shorter events, 0.0 us)
Async XLA Ops:
  0.7 1.6 copy-start.2
  2.2 0.9 copy-start.3
  29.5 1.3 copy-start
  144.8 2.9 %collective-permute-start = (bf16[2,128,2048]{2,1,0:T(8,128)(2,1)S(1)}, bf16[2,128,2048]{2,1,0:T(8,128)(2,1)}, u32[]{:S(2)}, u32[]{:S(2)}) collective-permute-start(bf16[2,128,2048]{2,1,0:T(8,128)(2,1)S(1)} %dynamic-slice_bitcast_fusion), channel_id=1, source_target_pairs={{0,1},{1,0},{2,3},{3,2},{4,5},{5,4},{6,7},{7,6},{8,9},{9,8},{10,11... | collective-permute-start | bytes 3145736 | tf_op jit(solution)/shard_map/ppermute | solution.py:466
  144.9 6.6 %copy-start.8 = (s32[3584]{0:T(1024)S(1)}, s32[3584]{0:T(1024)}, u32[]{:S(2)}) copy-start(s32[3584]{0:T(1024)} %param.9) | copy-start | bytes 43012
  145.0 6.6 %copy-start.1 = (bf16[512,2048]{1,0:T(8,128)(2,1)S(1)}, bf16[512,2048]{1,0:T(8,128)(2,1)}, u32[]{:S(2)}) copy-start(bf16[512,2048]{1,0:T(8,128)(2,1)} %copy-done) | copy-start | bytes 6291460
  150.5 14.3 %collective-permute-start.1 = (bf16[128,2048]{1,0:T(8,128)(2,1)}, bf16[128,2048]{1,0:T(8,128)(2,1)}, u32[]{:S(2)}, u32[]{:S(2)}) collective-permute-start(bf16[128,2048]{1,0:T(8,128)(2,1)} %dynamic-slice_bitcast_fusion.1), channel_id=1, source_target_pairs={{0,2},{1,3},{2,0},{3,1},{4,6},{5,7},{6,4},{7,5},{8,10},{9,11},{10,... | collective-permute-start | bytes 1572872 | tf_op jit(solution)/shard_map/ppermute | solution.py:466
  154.0 2.6 %copy-start.5 = (bf16[512,2048]{0,1:T(8,128)(2,1)S(1)}, bf16[512,2048]{0,1:T(8,128)(2,1)}, u32[]{:S(2)}) copy-start(bf16[512,2048]{0,1:T(8,128)(2,1)} %copy.9) | copy-start | bytes 6291460
  156.5 1.2 copy-start.6
  157.7 11.2 %copy-start.4 = (bf16[512,3584]{1,0:T(8,128)(2,1)S(1)}, bf16[512,3584]{1,0:T(8,128)(2,1)}, u32[]{:S(2)}) copy-start(bf16[512,3584]{1,0:T(8,128)(2,1)} %get-tuple-element.15.mine_ref) | copy-start | bytes 11010052
  165.9 28.7 %collective-permute-start.2 = (bf16[128,2048]{1,0:T(8,128)(2,1)S(1)}, bf16[128,2048]{1,0:T(8,128)(2,1)S(1)}, u32[]{:S(2)}, u32[]{:S(2)}) collective-permute-start(bf16[128,2048]{1,0:T(8,128)(2,1)S(1)} %fusion.1), channel_id=1, source_target_pairs={{0,0},{1,8},{2,16},{3,24},{8,1},{9,9},{10,17},{11,25},{16,2},{17,1... | collective-permute-start | bytes 1572872 | tf_op jit(solution)/shard_map/ppermute | solution.py:535
  168.9 25.7 %copy-start.7 = (bf16[128,3584]{1,0:T(8,128)(2,1)S(1)}, bf16[128,3584]{1,0:T(8,128)(2,1)}, u32[]{:S(2)}) copy-start(bf16[128,3584]{1,0:T(8,128)(2,1)} %get-tuple-element.20) | copy-start | bytes 2752516
